TPU v7x, 32 devices: a whole 2x2x4 slice. The times are simulated.
32 devices in a mesh: grp: 2 (over y), cell: 4 (over z), snap: 2 (over x), var: 2 (over core).
Axes of the slice: x: 2, y: 2, z: 4, core: 2. Of those that a mesh axis runs over, the one named last changes fastest.
Arguments:
- q_true: bfloat16 [64, 10, 2048], P(('snap', 'var'), 'grp', 'cell'), parts along dimension 1, may hold values from -6 to 6
- coeffs: bfloat16 [64, 256], P(('snap', 'var'), 'grp'), parts along dimension 1, may hold values from -0.5 to 0.5
- basis: bfloat16 [128, 10, 2048], P(('snap', 'var'), 'grp', 'cell'), parts along dimension 1, may hold values from -6 to 6
- weights: float32 [10, 2048], P('grp', 'cell'), parts along dimension 0, may hold values from 0.0029646354 to 0.029646354
- geometry: float32 [12, 2048], P('grp', 'cell'), parts along dimension 0, may hold values from 0.2 to 1
- neighbors: int32 [12, 2048], P('grp', 'cell'), parts along dimension 0, may hold values from 0 to 767, as said below
- send_rows: int32 [4, 4, 128], P('cell', 'grp'), parts along dimension 1, may hold values from 0 to 511, as said below
- block_count: int32 [4, 2], P('cell', 'grp'), parts along dimension 1, may hold values from 2 to 4
Outputs:
- closure: float32 [64, 256], P(('snap', 'var'), 'grp'), parts along dimension 1
There are 2 independent parts, one for each index of `grp`. A program takes and returns all parts, laid end to end along the dimension named above; each array names one. Nothing has to cross between parts.
Inputs may be any that keep to these rules, and one draw needn't show every extreme that they name: neighbors[k, c] indexes a list made of the 512 cells of c's own cell shard, then the 128 cells received from the shard before, then the 128 cells received from the shard after. `send_rows`: indices local to the sending cell shard.
All inputs are finite; a program needn't handle non-finite values.
Results may differ from a plain program's by a relative error of at most 0.00091.
Values may be sent and summed in bfloat16 or wider, within the bound.
A program may use at most 64 MiB of HBM per device.

v0:
```python
import math
import jax
import jax.numpy as jnp
from jax import lax
from jax.sharding import PartitionSpec as P

BLOCK = 128


def from_behind(shard, axis, by):
    peers = lax.axis_size(axis)
    pairs = [(i, i + by) for i in range(peers) if 0 <= i + by < peers]
    return lax.ppermute(shard, axis, pairs)


def face_flux(extended, geometry, neighbors):
    cell_count = geometry.shape[1]
    var_count = extended.shape[1]
    own_cells = extended[:, :, :cell_count]
    product = extended * extended[:, 1:2, :]
    own_product = product[:, :, :cell_count]
    stacked = jnp.concatenate([extended, product], axis=1)
    running = jnp.zeros(own_cells.shape, jnp.float32)
    for face_index in range(geometry.shape[0]):
        taken = jnp.take(stacked, neighbors[face_index], axis=2)
        beside = taken[:, :var_count]
        beside_product = taken[:, var_count:]
        running = running + geometry[face_index] * (
            0.5 * (own_product + beside_product) - 0.5 * (beside - own_cells)
        )
    return running


def local(q_true, coeffs, basis, weights, geometry, neighbors, send_rows, block_count):
    snap_count, var_count, cell_count = q_true.shape
    send_lists = send_rows[0]

    def rim_rows(field):
        return (jnp.take(field, send_lists[0], axis=2), jnp.take(field, send_lists[1], axis=2))

    true_to_prev, true_to_next = rim_rows(q_true)
    whole_basis = lax.all_gather(basis, ("snap", "var"), axis=0, tiled=True)
    basis_flat = whole_basis.reshape(whole_basis.shape[0], var_count * cell_count)
    rebuilt_sum = jnp.dot(coeffs, basis_flat, preferred_element_type=jnp.float32)
    rebuilt = rebuilt_sum.astype(jnp.bfloat16).reshape(snap_count, var_count, cell_count)
    rebuilt_to_prev, rebuilt_to_next = rim_rows(rebuilt)
    true_from_prev = from_behind(true_to_next, "cell", 1)
    true_from_next = from_behind(true_to_prev, "cell", -1)
    rebuilt_from_prev = from_behind(rebuilt_to_next, "cell", 1)
    rebuilt_from_next = from_behind(rebuilt_to_prev, "cell", -1)
    true_ext = jnp.concatenate([q_true, true_from_prev, true_from_next], axis=2)
    rebuilt_ext = jnp.concatenate([rebuilt, rebuilt_from_prev, rebuilt_from_next], axis=2)
    positions = jnp.arange(cell_count, dtype=jnp.int32)
    live = (positions < block_count[0, 0] * BLOCK).astype(jnp.float32)
    group = math.gcd(snap_count, 8)
    ext_count = true_ext.shape[2]

    def snap_block(pair):
        true_part, rebuilt_part = pair
        flux_true = face_flux(true_part.astype(jnp.float32), geometry, neighbors)
        flux_rebuilt = face_flux(rebuilt_part.astype(jnp.float32), geometry, neighbors)
        return (weights * live * (flux_true - flux_rebuilt)).astype(jnp.bfloat16)

    true_groups = true_ext.reshape(snap_count // group, group, var_count, ext_count)
    rebuilt_groups = rebuilt_ext.reshape(snap_count // group, group, var_count, ext_count)
    weighted = lax.map(snap_block, (true_groups, rebuilt_groups))
    weighted_flat = weighted.reshape(snap_count, var_count * cell_count)
    contract = (((1,), (1,)), ((), ()))
    closure_part = lax.dot_general(
        weighted_flat, basis_flat, contract, preferred_element_type=jnp.float32
    )
    return lax.psum(closure_part, "cell")


def solution(mesh):
    in_specs = (
        P(("snap", "var"), "grp", "cell"),
        P(("snap", "var"), "grp"),
        P(("snap", "var"), "grp", "cell"),
        P("grp", "cell"),
        P("grp", "cell"),
        P("grp", "cell"),
        P("cell", "grp", None),
        P("cell", "grp"),
    )
    out_specs = P(("snap", "var"), "grp")
    return jax.shard_map(local, mesh=mesh, in_specs=in_specs, out_specs=out_specs, check_vma=False)
```

profile of v0, /device:TPU:0, one launch (start us, length us, event | category | flops | bytes accessed | tf_op | source)
XLA Modules:
  0.0 230.5 jit_solution(12883758674813576312)
XLA Ops:
  0.8 9.7 %all_gather.3 = bf16[128,5,512]{2,0,1:T(8,128)(2,1)S(1)} all-gather(bf16[32,5,512]{2,0,1:T(8,128)(2,1)} %param.16), channel_id=1, replica_groups=mesh['grp'=2,'cell'=4,'snap'=2,'var'=2] {'snap','var'}, dimensions={0}, use_global_device_ids=true | all-gather | bytes 819200 | tf_op jit(solution)/shard_map/all_gather | solution.py:42
  15.2 3.5 %collective-permute-start = (bf16[16,5,128]{0,1,2:T(8,128)(2,1)}, bf16[16,5,128]{0,1,2:T(8,128)(2,1)S(1)}, u32[]{:S(2)}, u32[]{:S(2)}) collective-permute-start(bf16[16,5,128]{0,1,2:T(8,128)(2,1)} %get-tuple-element.158), channel_id=1, source_target_pairs={{0,4},{4,8},{8,12},{1,5},{5,9},{9,13},{2,6},{6,10},{10,14},{3,7},{... | collective-permute-start | bytes 61448 | tf_op jit(solution)/shard_map/ppermute | solution.py:13
  21.6 4.6 %collective-permute-start.2 = (bf16[16,5,128]{0,1,2:T(8,128)(2,1)}, bf16[16,5,128]{0,1,2:T(8,128)(2,1)S(1)}, u32[]{:S(2)}, u32[]{:S(2)}) collective-permute-start(bf16[16,5,128]{0,1,2:T(8,128)(2,1)} %get-tuple-element.157), channel_id=1, source_target_pairs={{0,4},{4,8},{8,12},{1,5},{5,9},{9,13},{2,6},{6,10},{10,14},{3,7},{... | collective-permute-start | bytes 61448 | tf_op jit(solution)/shard_map/ppermute | solution.py:13
  28.3 2.4 %collective-permute-done.1 = bf16[16,5,128]{0,1,2:T(8,128)(2,1)S(1)} collective-permute-done((bf16[16,5,128]{0,1,2:T(8,128)(2,1)S(1)}, bf16[16,5,128]{0,1,2:T(8,128)(2,1)S(1)}, u32[]{:S(2)}, u32[]{:S(2)}) %collective-permute-start.1) | collective-permute-done | bytes 20512 | tf_op jit(solution)/shard_map/ppermute | solution.py:13
  32.1 4.0 %collective-permute-done.3 = bf16[16,5,128]{0,1,2:T(8,128)(2,1)S(1)} collective-permute-done((bf16[16,5,128]{0,1,2:T(8,128)(2,1)S(1)}, bf16[16,5,128]{0,1,2:T(8,128)(2,1)S(1)}, u32[]{:S(2)}, u32[]{:S(2)}) %collective-permute-start.3) | collective-permute-done | bytes 20512 | tf_op jit(solution)/shard_map/ppermute | solution.py:13
  36.9 181.6 %while.11 = (s32[]{:T(128)}, bf16[2,8,5,512]{3,1,2,0:T(8,128)(2,1)}, f32[5,512]{1,0:T(8,128)S(1)}, f32[6,512]{1,0:T(8,128)}, bf16[2,8,5,768]{3,1,0,2:T(8,128)(2,...) while((s32[]{:T(128)}, ...), condition=%wide.region_1.4_spmd.clone, body=%wide.region_0.3_spmd.clone.sunk | while | flops 2576898 | bytes 26133308 | solution.py:66
  47.5 2.2 copy.153
  49.7 2.8 %gather_fusion.11 = f32[512,8,10]{2,1,0:T(8,128)} fusion(f32[8,10,768]{1,0,2:T(8,128)S(1)} %copy.153, s32[1024]{0:T(1024)} %pad_clamp_fusion.19), kind=kCustom, calls=%fused_computation.10.clone.clone.1 | custom fusion | bytes 329728 | tf_op jit(solution)/shard_map/while/body/eval_jaxpr/jit(_take)/gather | solution.py:25
  52.5 2.9 %copy.164 = f32[512,8,10]{0,1,2:T(8,128)} copy(f32[512,8,10]{2,1,0:T(8,128)} %gather_fusion.11) | data formatting | bytes 327680 | tf_op jit(solution)/shard_map/while/body/eval_jaxpr/jit(_take)/gather | solution.py:25
  55.4 2.7 %gather_fusion.9 = f32[512,8,10]{2,1,0:T(8,128)} fusion(f32[8,10,768]{1,0,2:T(8,128)S(1)} %copy.153, s32[1024]{0:T(1024)S(1)} %pad_clamp_fusion.18), kind=kCustom, calls=%fused_computation.11.clone.clone.1 | custom fusion | bytes 329728 | tf_op jit(solution)/shard_map/while/body/eval_jaxpr/jit(_take)/gather | solution.py:25
  58.1 2.9 %copy.162 = f32[512,8,10]{0,1,2:T(8,128)} copy(f32[512,8,10]{2,1,0:T(8,128)} %gather_fusion.9) | data formatting | bytes 327680 | tf_op jit(solution)/shard_map/while/body/eval_jaxpr/jit(_take)/gather | solution.py:25
  61.0 2.7 %gather_fusion.7 = f32[512,8,10]{2,1,0:T(8,128)} fusion(f32[8,10,768]{1,0,2:T(8,128)S(1)} %copy.153, s32[1024]{0:T(1024)S(1)} %pad_clamp_fusion.17), kind=kCustom, calls=%fused_computation.12.clone.clone.1 | custom fusion | bytes 329728 | tf_op jit(solution)/shard_map/while/body/eval_jaxpr/jit(_take)/gather | solution.py:25
  63.6 2.9 %copy.160 = f32[512,8,10]{0,1,2:T(8,128)} copy(f32[512,8,10]{2,1,0:T(8,128)} %gather_fusion.7) | data formatting | bytes 327680 | tf_op jit(solution)/shard_map/while/body/eval_jaxpr/jit(_take)/gather | solution.py:25
  66.5 2.7 %gather_fusion.5 = f32[512,8,10]{2,1,0:T(8,128)} fusion(f32[8,10,768]{1,0,2:T(8,128)S(1)} %copy.153, s32[1024]{0:T(1024)S(1)} %pad_clamp_fusion.16), kind=kCustom, calls=%fused_computation.13.clone.clone.1 | custom fusion | bytes 329728 | tf_op jit(solution)/shard_map/while/body/eval_jaxpr/jit(_take)/gather | solution.py:25
  69.2 2.9 %copy.158 = f32[512,8,10]{0,1,2:T(8,128)} copy(f32[512,8,10]{2,1,0:T(8,128)} %gather_fusion.5) | data formatting | bytes 327680 | tf_op jit(solution)/shard_map/while/body/eval_jaxpr/jit(_take)/gather | solution.py:25
  72.1 2.7 %gather_fusion.3 = f32[512,8,10]{2,1,0:T(8,128)} fusion(f32[8,10,768]{1,0,2:T(8,128)S(1)} %copy.153, s32[1024]{0:T(1024)S(1)} %pad_clamp_fusion.15), kind=kCustom, calls=%fused_computation.14.clone.clone.1 | custom fusion | bytes 329728 | tf_op jit(solution)/shard_map/while/body/eval_jaxpr/jit(_take)/gather | solution.py:25
  74.8 2.9 %copy.156 = f32[512,8,10]{0,1,2:T(8,128)} copy(f32[512,8,10]{2,1,0:T(8,128)} %gather_fusion.3) | data formatting | bytes 327680 | tf_op jit(solution)/shard_map/while/body/eval_jaxpr/jit(_take)/gather | solution.py:25
  77.7 2.7 %gather_fusion.1 = f32[512,8,10]{2,1,0:T(8,128)} fusion(f32[8,10,768]{1,0,2:T(8,128)S(1)} %copy.153, s32[1024]{0:T(1024)S(1)} %pad_clamp_fusion.14), kind=kCustom, calls=%fused_computation.15.clone.clone.1 | custom fusion | bytes 329728 | tf_op jit(solution)/shard_map/while/body/eval_jaxpr/jit(_take)/gather | solution.py:25
  80.3 2.9 %copy.154 = f32[512,8,10]{0,1,2:T(8,128)} copy(f32[512,8,10]{2,1,0:T(8,128)} %gather_fusion.1) | data formatting | bytes 327680 | tf_op jit(solution)/shard_map/while/body/eval_jaxpr/jit(_take)/gather | solution.py:25
  83.2 2.2 copy.151
  85.4 2.8 %gather_fusion.10 = f32[512,8,10]{2,1,0:T(8,128)} fusion(f32[8,10,768]{1,0,2:T(8,128)S(1)} %copy.151, s32[1024]{0:T(1024)} %pad_clamp_fusion.19), kind=kCustom, calls=%fused_computation.1.clone.clone.1 | custom fusion | bytes 329728 | tf_op jit(solution)/shard_map/while/body/eval_jaxpr/jit(_take)/gather | solution.py:25
  88.2 2.9 %copy.163 = f32[512,8,10]{0,1,2:T(8,128)} copy(f32[512,8,10]{2,1,0:T(8,128)} %gather_fusion.10) | data formatting | bytes 327680 | tf_op jit(solution)/shard_map/while/body/eval_jaxpr/jit(_take)/gather | solution.py:25
  92.9 2.7 %gather_fusion.8 = f32[512,8,10]{2,1,0:T(8,128)} fusion(f32[8,10,768]{1,0,2:T(8,128)S(1)} %copy.151, s32[1024]{0:T(1024)S(1)} %pad_clamp_fusion.18), kind=kCustom, calls=%fused_computation.5.clone.clone.1 | custom fusion | bytes 329728 | tf_op jit(solution)/shard_map/while/body/eval_jaxpr/jit(_take)/gather | solution.py:25
  95.5 2.9 %copy.161 = f32[512,8,10]{0,1,2:T(8,128)} copy(f32[512,8,10]{2,1,0:T(8,128)} %gather_fusion.8) | data formatting | bytes 327680 | tf_op jit(solution)/shard_map/while/body/eval_jaxpr/jit(_take)/gather | solution.py:25
  98.4 1.8 select_bitcast_fusion.26
  100.2 2.7 %gather_fusion.6 = f32[512,8,10]{2,1,0:T(8,128)} fusion(f32[8,10,768]{1,0,2:T(8,128)S(1)} %copy.151, s32[1024]{0:T(1024)S(1)} %pad_clamp_fusion.17), kind=kCustom, calls=%fused_computation.6.clone.clone.1 | custom fusion | bytes 329728 | tf_op jit(solution)/shard_map/while/body/eval_jaxpr/jit(_take)/gather | solution.py:25
  102.9 2.9 %copy.159 = f32[512,8,10]{0,1,2:T(8,128)} copy(f32[512,8,10]{2,1,0:T(8,128)} %gather_fusion.6) | data formatting | bytes 327680 | tf_op jit(solution)/shard_map/while/body/eval_jaxpr/jit(_take)/gather | solution.py:25
  105.8 1.8 select_bitcast_fusion.25
  107.6 2.7 %gather_fusion.4 = f32[512,8,10]{2,1,0:T(8,128)} fusion(f32[8,10,768]{1,0,2:T(8,128)S(1)} %copy.151, s32[1024]{0:T(1024)S(1)} %pad_clamp_fusion.16), kind=kCustom, calls=%fused_computation.7.clone.clone.1 | custom fusion | bytes 329728 | tf_op jit(solution)/shard_map/while/body/eval_jaxpr/jit(_take)/gather | solution.py:25
  110.3 2.9 %copy.157 = f32[512,8,10]{0,1,2:T(8,128)} copy(f32[512,8,10]{2,1,0:T(8,128)} %gather_fusion.4) | data formatting | bytes 327680 | tf_op jit(solution)/shard_map/while/body/eval_jaxpr/jit(_take)/gather | solution.py:25
  113.2 1.8 select_bitcast_fusion.24
  114.9 2.7 %gather_fusion.2 = f32[512,8,10]{2,1,0:T(8,128)} fusion(f32[8,10,768]{1,0,2:T(8,128)S(1)} %copy.151, s32[1024]{0:T(1024)S(1)} %pad_clamp_fusion.15), kind=kCustom, calls=%fused_computation.8.clone.clone.1 | custom fusion | bytes 329728 | tf_op jit(solution)/shard_map/while/body/eval_jaxpr/jit(_take)/gather | solution.py:25
  117.6 2.9 %copy.155 = f32[512,8,10]{0,1,2:T(8,128)} copy(f32[512,8,10]{2,1,0:T(8,128)} %gather_fusion.2) | data formatting | bytes 327680 | tf_op jit(solution)/shard_map/while/body/eval_jaxpr/jit(_take)/gather | solution.py:25
  120.5 2.7 %gather_fusion = f32[512,8,10]{2,1,0:T(8,128)} fusion(f32[8,10,768]{1,0,2:T(8,128)S(1)} %copy.151, s32[1024]{0:T(1024)S(1)} %pad_clamp_fusion.14), kind=kCustom, calls=%fused_computation.9.clone.clone.1 | custom fusion | bytes 329728 | tf_op jit(solution)/shard_map/while/body/eval_jaxpr/jit(_take)/gather | solution.py:25
  123.4 2.4 %copy.152 = f32[512,8,10]{0,1,2:T(8,128)S(1)} copy(f32[512,8,10]{2,1,0:T(8,128)} %gather_fusion) | data formatting | bytes 327680 | tf_op jit(solution)/shard_map/while/body/eval_jaxpr/jit(_take)/gather | solution.py:25
  138.3 2.2 copy.153
  140.5 2.8 %gather_fusion.11 = f32[512,8,10]{2,1,0:T(8,128)} fusion(f32[8,10,768]{1,0,2:T(8,128)S(1)} %copy.153, s32[1024]{0:T(1024)} %pad_clamp_fusion.19), kind=kCustom, calls=%fused_computation.10.clone.clone.1 | custom fusion | bytes 329728 | tf_op jit(solution)/shard_map/while/body/eval_jaxpr/jit(_take)/gather | solution.py:25
  143.3 2.9 %copy.164 = f32[512,8,10]{0,1,2:T(8,128)} copy(f32[512,8,10]{2,1,0:T(8,128)} %gather_fusion.11) | data formatting | bytes 327680 | tf_op jit(solution)/shard_map/while/body/eval_jaxpr/jit(_take)/gather | solution.py:25
  146.2 2.7 %gather_fusion.9 = f32[512,8,10]{2,1,0:T(8,128)} fusion(f32[8,10,768]{1,0,2:T(8,128)S(1)} %copy.153, s32[1024]{0:T(1024)S(1)} %pad_clamp_fusion.18), kind=kCustom, calls=%fused_computation.11.clone.clone.1 | custom fusion | bytes 329728 | tf_op jit(solution)/shard_map/while/body/eval_jaxpr/jit(_take)/gather | solution.py:25
  148.9 2.9 %copy.162 = f32[512,8,10]{0,1,2:T(8,128)} copy(f32[512,8,10]{2,1,0:T(8,128)} %gather_fusion.9) | data formatting | bytes 327680 | tf_op jit(solution)/shard_map/while/body/eval_jaxpr/jit(_take)/gather | solution.py:25
  151.7 2.7 %gather_fusion.7 = f32[512,8,10]{2,1,0:T(8,128)} fusion(f32[8,10,768]{1,0,2:T(8,128)S(1)} %copy.153, s32[1024]{0:T(1024)S(1)} %pad_clamp_fusion.17), kind=kCustom, calls=%fused_computation.12.clone.clone.1 | custom fusion | bytes 329728 | tf_op jit(solution)/shard_map/while/body/eval_jaxpr/jit(_take)/gather | solution.py:25
  154.4 2.9 %copy.160 = f32[512,8,10]{0,1,2:T(8,128)} copy(f32[512,8,10]{2,1,0:T(8,128)} %gather_fusion.7) | data formatting | bytes 327680 | tf_op jit(solution)/shard_map/while/body/eval_jaxpr/jit(_take)/gather | solution.py:25
  157.3 2.7 %gather_fusion.5 = f32[512,8,10]{2,1,0:T(8,128)} fusion(f32[8,10,768]{1,0,2:T(8,128)S(1)} %copy.153, s32[1024]{0:T(1024)S(1)} %pad_clamp_fusion.16), kind=kCustom, calls=%fused_computation.13.clone.clone.1 | custom fusion | bytes 329728 | tf_op jit(solution)/shard_map/while/body/eval_jaxpr/jit(_take)/gather | solution.py:25
  160.0 2.9 %copy.158 = f32[512,8,10]{0,1,2:T(8,128)} copy(f32[512,8,10]{2,1,0:T(8,128)} %gather_fusion.5) | data formatting | bytes 327680 | tf_op jit(solution)/shard_map/while/body/eval_jaxpr/jit(_take)/gather | solution.py:25
  162.9 2.7 %gather_fusion.3 = f32[512,8,10]{2,1,0:T(8,128)} fusion(f32[8,10,768]{1,0,2:T(8,128)S(1)} %copy.153, s32[1024]{0:T(1024)S(1)} %pad_clamp_fusion.15), kind=kCustom, calls=%fused_computation.14.clone.clone.1 | custom fusion | bytes 329728 | tf_op jit(solution)/shard_map/while/body/eval_jaxpr/jit(_take)/gather | solution.py:25
  165.6 2.9 %copy.156 = f32[512,8,10]{0,1,2:T(8,128)} copy(f32[512,8,10]{2,1,0:T(8,128)} %gather_fusion.3) | data formatting | bytes 327680 | tf_op jit(solution)/shard_map/while/body/eval_jaxpr/jit(_take)/gather | solution.py:25
  168.4 2.7 %gather_fusion.1 = f32[512,8,10]{2,1,0:T(8,128)} fusion(f32[8,10,768]{1,0,2:T(8,128)S(1)} %copy.153, s32[1024]{0:T(1024)S(1)} %pad_clamp_fusion.14), kind=kCustom, calls=%fused_computation.15.clone.clone.1 | custom fusion | bytes 329728 | tf_op jit(solution)/shard_map/while/body/eval_jaxpr/jit(_take)/gather | solution.py:25
  171.1 2.9 %copy.154 = f32[512,8,10]{0,1,2:T(8,128)} copy(f32[512,8,10]{2,1,0:T(8,128)} %gather_fusion.1) | data formatting | bytes 327680 | tf_op jit(solution)/shard_map/while/body/eval_jaxpr/jit(_take)/gather | solution.py:25
  174.0 2.2 copy.151
  176.2 2.8 %gather_fusion.10 = f32[512,8,10]{2,1,0:T(8,128)} fusion(f32[8,10,768]{1,0,2:T(8,128)S(1)} %copy.151, s32[1024]{0:T(1024)} %pad_clamp_fusion.19), kind=kCustom, calls=%fused_computation.1.clone.clone.1 | custom fusion | bytes 329728 | tf_op jit(solution)/shard_map/while/body/eval_jaxpr/jit(_take)/gather | solution.py:25
  179.0 2.9 %copy.163 = f32[512,8,10]{0,1,2:T(8,128)} copy(f32[512,8,10]{2,1,0:T(8,128)} %gather_fusion.10) | data formatting | bytes 327680 | tf_op jit(solution)/shard_map/while/body/eval_jaxpr/jit(_take)/gather | solution.py:25
  183.6 2.7 %gather_fusion.8 = f32[512,8,10]{2,1,0:T(8,128)} fusion(f32[8,10,768]{1,0,2:T(8,128)S(1)} %copy.151, s32[1024]{0:T(1024)S(1)} %pad_clamp_fusion.18), kind=kCustom, calls=%fused_computation.5.clone.clone.1 | custom fusion | bytes 329728 | tf_op jit(solution)/shard_map/while/body/eval_jaxpr/jit(_take)/gather | solution.py:25
  186.3 2.9 %copy.161 = f32[512,8,10]{0,1,2:T(8,128)} copy(f32[512,8,10]{2,1,0:T(8,128)} %gather_fusion.8) | data formatting | bytes 327680 | tf_op jit(solution)/shard_map/while/body/eval_jaxpr/jit(_take)/gather | solution.py:25
  189.2 1.8 select_bitcast_fusion.26
  191.0 2.7 %gather_fusion.6 = f32[512,8,10]{2,1,0:T(8,128)} fusion(f32[8,10,768]{1,0,2:T(8,128)S(1)} %copy.151, s32[1024]{0:T(1024)S(1)} %pad_clamp_fusion.17), kind=kCustom, calls=%fused_computation.6.clone.clone.1 | custom fusion | bytes 329728 | tf_op jit(solution)/shard_map/while/body/eval_jaxpr/jit(_take)/gather | solution.py:25
  193.7 2.9 %copy.159 = f32[512,8,10]{0,1,2:T(8,128)} copy(f32[512,8,10]{2,1,0:T(8,128)} %gather_fusion.6) | data formatting | bytes 327680 | tf_op jit(solution)/shard_map/while/body/eval_jaxpr/jit(_take)/gather | solution.py:25
  196.6 1.8 select_bitcast_fusion.25
  198.3 2.7 %gather_fusion.4 = f32[512,8,10]{2,1,0:T(8,128)} fusion(f32[8,10,768]{1,0,2:T(8,128)S(1)} %copy.151, s32[1024]{0:T(1024)S(1)} %pad_clamp_fusion.16), kind=kCustom, calls=%fused_computation.7.clone.clone.1 | custom fusion | bytes 329728 | tf_op jit(solution)/shard_map/while/body/eval_jaxpr/jit(_take)/gather | solution.py:25
  201.1 2.9 %copy.157 = f32[512,8,10]{0,1,2:T(8,128)} copy(f32[512,8,10]{2,1,0:T(8,128)} %gather_fusion.4) | data formatting | bytes 327680 | tf_op jit(solution)/shard_map/while/body/eval_jaxpr/jit(_take)/gather | solution.py:25
  205.7 2.7 %gather_fusion.2 = f32[512,8,10]{2,1,0:T(8,128)} fusion(f32[8,10,768]{1,0,2:T(8,128)S(1)} %copy.151, s32[1024]{0:T(1024)S(1)} %pad_clamp_fusion.15), kind=kCustom, calls=%fused_computation.8.clone.clone.1 | custom fusion | bytes 329728 | tf_op jit(solution)/shard_map/while/body/eval_jaxpr/jit(_take)/gather | solution.py:25
  208.4 2.9 %copy.155 = f32[512,8,10]{0,1,2:T(8,128)} copy(f32[512,8,10]{2,1,0:T(8,128)} %gather_fusion.2) | data formatting | bytes 327680 | tf_op jit(solution)/shard_map/while/body/eval_jaxpr/jit(_take)/gather | solution.py:25
  211.3 2.7 %gather_fusion = f32[512,8,10]{2,1,0:T(8,128)} fusion(f32[8,10,768]{1,0,2:T(8,128)S(1)} %copy.151, s32[1024]{0:T(1024)S(1)} %pad_clamp_fusion.14), kind=kCustom, calls=%fused_computation.9.clone.clone.1 | custom fusion | bytes 329728 | tf_op jit(solution)/shard_map/while/body/eval_jaxpr/jit(_take)/gather | solution.py:25
  214.1 2.4 %copy.152 = f32[512,8,10]{0,1,2:T(8,128)S(1)} copy(f32[512,8,10]{2,1,0:T(8,128)} %gather_fusion) | data formatting | bytes 327680 | tf_op jit(solution)/shard_map/while/body/eval_jaxpr/jit(_take)/gather | solution.py:25
  219.8 10.7 %psum.7 = f32[16,128]{1,0:T(8,128)} all-reduce(f32[16,128]{1,0:T(8,128)S(1)} %fusion.66), channel_id=1, replica_groups=mesh['grp'=2,'cell'=4,'snap'=2,'var'=2] {'cell'}, use_global_device_ids=true, to_apply=%region_2.5 | all-reduce | flops 2048 | bytes 16384 | tf_op jit(solution)/shard_map/psum | solution.py:72
  (201 shorter events, 43.2 us)
Async XLA Ops:
  0.0 10.8 %copy-start = (bf16[16,128]{1,0:T(8,128)(2,1)S(1)}, bf16[16,128]{1,0:T(8,128)(2,1)}, u32[]{:S(2)}) copy-start(bf16[16,128]{1,0:T(8,128)(2,1)} %param.15) | copy-start | bytes 12292
  0.8 11.3 %copy-start.17 = (bf16[16,5,512]{2,0,1:T(8,128)(2,1)S(1)}, bf16[16,5,512]{2,0,1:T(8,128)(2,1)}, u32[]{:S(2)}) copy-start(bf16[16,5,512]{2,0,1:T(8,128)(2,1)} %param.14) | copy-start | bytes 245764
  10.8 4.4 %copy-start.14 = (bf16[128,5,512]{0,2,1:T(8,128)(2,1)}, bf16[128,5,512]{0,2,1:T(8,128)(2,1)S(1)}, u32[]{:S(2)}) copy-start(bf16[128,5,512]{0,2,1:T(8,128)(2,1)S(1)} %copy.124) | copy-start | bytes 1966084
  12.8 24.1 %copy-start.15 = (f32[5,512]{1,0:T(8,128)S(1)}, f32[5,512]{1,0:T(8,128)}, u32[]{:S(2)}) copy-start(f32[5,512]{1,0:T(8,128)} %param.17) | copy-start | bytes 30724
  15.2 12.9 %collective-permute-start = (bf16[16,5,128]{0,1,2:T(8,128)(2,1)}, bf16[16,5,128]{0,1,2:T(8,128)(2,1)S(1)}, u32[]{:S(2)}, u32[]{:S(2)}) collective-permute-start(bf16[16,5,128]{0,1,2:T(8,128)(2,1)} %get-tuple-element.158), channel_id=1, source_target_pairs={{0,4},{4,8},{8,12},{1,5},{5,9},{9,13},{2,6},{6,10},{10,14},{3,7},{... | collective-permute-start | bytes 61448 | tf_op jit(solution)/shard_map/ppermute | solution.py:13
  20.3 10.4 %collective-permute-start.1 = (bf16[16,5,128]{0,1,2:T(8,128)(2,1)S(1)}, bf16[16,5,128]{0,1,2:T(8,128)(2,1)S(1)}, u32[]{:S(2)}, u32[]{:S(2)}) collective-permute-start(bf16[16,5,128]{0,1,2:T(8,128)(2,1)S(1)} %get-tuple-element.160), channel_id=1, source_target_pairs={{4,0},{8,4},{12,8},{5,1},{9,5},{13,9},{6,2},{10,6},{14,10},{7,3},{... | collective-permute-start | bytes 61448 | tf_op jit(solution)/shard_map/ppermute | solution.py:13
  21.6 10.4 %collective-permute-start.2 = (bf16[16,5,128]{0,1,2:T(8,128)(2,1)}, bf16[16,5,128]{0,1,2:T(8,128)(2,1)S(1)}, u32[]{:S(2)}, u32[]{:S(2)}) collective-permute-start(bf16[16,5,128]{0,1,2:T(8,128)(2,1)} %get-tuple-element.157), channel_id=1, source_target_pairs={{0,4},{4,8},{8,12},{1,5},{5,9},{9,13},{2,6},{6,10},{10,14},{3,7},{... | collective-permute-start | bytes 61448 | tf_op jit(solution)/shard_map/ppermute | solution.py:13
  26.2 9.9 %collective-permute-start.3 = (bf16[16,5,128]{0,1,2:T(8,128)(2,1)S(1)}, bf16[16,5,128]{0,1,2:T(8,128)(2,1)S(1)}, u32[]{:S(2)}, u32[]{:S(2)}) collective-permute-start(bf16[16,5,128]{0,1,2:T(8,128)(2,1)S(1)} %get-tuple-element.159), channel_id=1, source_target_pairs={{4,0},{8,4},{12,8},{5,1},{9,5},{13,9},{6,2},{10,6},{14,10},{7,3},{... | collective-permute-start | bytes 61448 | tf_op jit(solution)/shard_map/ppermute | solution.py:13
  46.1 0.7 copy-start.1
  98.4 7.4 %copy-start.28 = (pred[512]{0:T(512)(128)(4,1)S(1)}, pred[512]{0:T(512)(128)(4,1)}, u32[]{:S(2)}) copy-start(pred[512]{0:T(512)(128)(4,1)} %compare_and_fusion.17) | copy-start | bytes 1540 | tf_op jit(solution)/shard_map/while
  105.8 7.4 %copy-start.27 = (pred[512]{0:T(512)(128)(4,1)S(1)}, pred[512]{0:T(512)(128)(4,1)}, u32[]{:S(2)}) copy-start(pred[512]{0:T(512)(128)(4,1)} %compare_and_fusion.16) | copy-start | bytes 1540 | tf_op jit(solution)/shard_map/while
  120.5 6.1 %copy-start.18 = (f32[1,512]{1,0:T(1,128)S(1)}, f32[1,512]{1,0:T(1,128)}, u32[]{:S(2)}) copy-start(f32[1,512]{1,0:T(1,128)} %get-tuple-element.261) | copy-start | bytes 6148 | tf_op jit(solution)/shard_map/while
  120.5 6.1 %copy-start.19 = (f32[1,512]{1,0:T(1,128)S(1)}, f32[1,512]{1,0:T(1,128)}, u32[]{:S(2)}) copy-start(f32[1,512]{1,0:T(1,128)} %get-tuple-element.251) | copy-start | bytes 6148 | tf_op jit(solution)/shard_map/while
  120.5 6.1 %copy-start.20 = (f32[1,512]{1,0:T(1,128)S(1)}, f32[1,512]{1,0:T(1,128)}, u32[]{:S(2)}) copy-start(f32[1,512]{1,0:T(1,128)} %get-tuple-element.253) | copy-start | bytes 6148 | tf_op jit(solution)/shard_map/while
  120.5 6.1 %copy-start.21 = (f32[1,512]{1,0:T(1,128)S(1)}, f32[1,512]{1,0:T(1,128)}, u32[]{:S(2)}) copy-start(f32[1,512]{1,0:T(1,128)} %get-tuple-element.255) | copy-start | bytes 6148 | tf_op jit(solution)/shard_map/while
  123.2 2.5 %copy-start.4 = (f32[512,8,10]{0,1,2:T(8,128)S(1)}, f32[512,8,10]{0,1,2:T(8,128)}, u32[]{:S(2)}) copy-start(f32[512,8,10]{0,1,2:T(8,128)} %copy.154) | copy-start | bytes 491524 | tf_op jit(solution)/shard_map/while
  123.2 3.3 %copy-start.3 = (f32[512,8,10]{0,1,2:T(8,128)S(1)}, f32[512,8,10]{0,1,2:T(8,128)}, u32[]{:S(2)}) copy-start(f32[512,8,10]{0,1,2:T(8,128)} %copy.156) | copy-start | bytes 491524 | tf_op jit(solution)/shard_map/while
  123.2 3.3 %copy-start.5 = (f32[512,8,10]{0,1,2:T(8,128)S(1)}, f32[512,8,10]{0,1,2:T(8,128)}, u32[]{:S(2)}) copy-start(f32[512,8,10]{0,1,2:T(8,128)} %copy.155) | copy-start | bytes 491524 | tf_op jit(solution)/shard_map/while
  123.2 3.3 %copy-start.26 = (pred[512]{0:T(512)(128)(4,1)S(1)}, pred[512]{0:T(512)(128)(4,1)}, u32[]{:S(2)}) copy-start(pred[512]{0:T(512)(128)(4,1)} %compare_and_fusion.15) | copy-start | bytes 1540 | tf_op jit(solution)/shard_map/while
  123.3 3.4 %copy-start.2 = (f32[8,5,768]{2,0,1:T(8,128)S(1)}, f32[8,5,768]{2,0,1:T(8,128)}, u32[]{:S(2)}) copy-start(f32[8,5,768]{2,0,1:T(8,128)} %copy-done.1) | copy-start | bytes 368644 | tf_op jit(solution)/shard_map/while
  123.3 3.4 %copy-start.6 = (f32[8,10,512]{2,0,1:T(8,128)S(1)}, f32[8,10,512]{2,0,1:T(8,128)}, u32[]{:S(2)}) copy-start(f32[8,10,512]{2,0,1:T(8,128)} %get-tuple-element.260) | copy-start | bytes 491524 | tf_op jit(solution)/shard_map/while
  123.3 3.4 %copy-start.7 = (f32[8,10,512]{2,0,1:T(8,128)S(1)}, f32[8,10,512]{2,0,1:T(8,128)}, u32[]{:S(2)}) copy-start(f32[8,10,512]{2,0,1:T(8,128)} %get-tuple-element.249) | copy-start | bytes 491524 | tf_op jit(solution)/shard_map/while
  123.3 3.4 %copy-start.8 = (f32[8,10,512]{2,0,1:T(8,128)S(1)}, f32[8,10,512]{2,0,1:T(8,128)}, u32[]{:S(2)}) copy-start(f32[8,10,512]{2,0,1:T(8,128)} %get-tuple-element.258) | copy-start | bytes 491524 | tf_op jit(solution)/shard_map/while
  123.3 3.4 %copy-start.9 = (f32[8,10,512]{2,0,1:T(8,128)S(1)}, f32[8,10,512]{2,0,1:T(8,128)}, u32[]{:S(2)}) copy-start(f32[8,10,512]{2,0,1:T(8,128)} %get-tuple-element.247) | copy-start | bytes 491524 | tf_op jit(solution)/shard_map/while
  123.3 3.4 %copy-start.10 = (f32[8,10,512]{2,0,1:T(8,128)S(1)}, f32[8,10,512]{2,0,1:T(8,128)}, u32[]{:S(2)}) copy-start(f32[8,10,512]{2,0,1:T(8,128)} %get-tuple-element.256) | copy-start | bytes 491524 | tf_op jit(solution)/shard_map/while
  123.3 3.4 %copy-start.11 = (f32[8,10,512]{2,0,1:T(8,128)S(1)}, f32[8,10,512]{2,0,1:T(8,128)}, u32[]{:S(2)}) copy-start(f32[8,10,512]{2,0,1:T(8,128)} %get-tuple-element.245) | copy-start | bytes 491524 | tf_op jit(solution)/shard_map/while
  123.3 3.4 %copy-start.12 = (f32[8,10,512]{2,0,1:T(8,128)S(1)}, f32[8,10,512]{2,0,1:T(8,128)}, u32[]{:S(2)}) copy-start(f32[8,10,512]{2,0,1:T(8,128)} %get-tuple-element.254) | copy-start | bytes 491524 | tf_op jit(solution)/shard_map/while
  123.3 3.4 %copy-start.13 = (f32[8,10,512]{2,0,1:T(8,128)S(1)}, f32[8,10,512]{2,0,1:T(8,128)}, u32[]{:S(2)}) copy-start(f32[8,10,512]{2,0,1:T(8,128)} %get-tuple-element.243) | copy-start | bytes 491524 | tf_op jit(solution)/shard_map/while
  123.3 3.4 %copy-start.22 = (f32[1,512]{1,0:T(1,128)S(1)}, f32[1,512]{1,0:T(1,128)}, u32[]{:S(2)}) copy-start(f32[1,512]{1,0:T(1,128)} %get-tuple-element.257) | copy-start | bytes 6148 | tf_op jit(solution)/shard_map/while
  123.4 3.4 %copy-start.23 = (f32[1,512]{1,0:T(1,128)S(1)}, f32[1,512]{1,0:T(1,128)}, u32[]{:S(2)}) copy-start(f32[1,512]{1,0:T(1,128)} %get-tuple-element.259) | copy-start | bytes 6148 | tf_op jit(solution)/shard_map/while
  123.4 3.4 %copy-start.24 = (bf16[2,8,5,512]{3,1,2,0:T(8,128)(2,1)S(1)}, bf16[2,8,5,512]{3,1,2,0:T(8,128)(2,1)}, u32[]{:S(2)}) copy-start(bf16[2,8,5,512]{3,1,2,0:T(8,128)(2,1)} %get-tuple-element.272) | copy-start | bytes 245764 | tf_op jit(solution)/shard_map/while
  125.8 1.9 copy-start.16
  127.0 0.6 copy-start.25
  136.8 0.7 copy-start.1
  189.2 7.4 %copy-start.28 = (pred[512]{0:T(512)(128)(4,1)S(1)}, pred[512]{0:T(512)(128)(4,1)}, u32[]{:S(2)}) copy-start(pred[512]{0:T(512)(128)(4,1)} %compare_and_fusion.17) | copy-start | bytes 1540 | tf_op jit(solution)/shard_map/while
  196.6 7.4 %copy-start.27 = (pred[512]{0:T(512)(128)(4,1)S(1)}, pred[512]{0:T(512)(128)(4,1)}, u32[]{:S(2)}) copy-start(pred[512]{0:T(512)(128)(4,1)} %compare_and_fusion.16) | copy-start | bytes 1540 | tf_op jit(solution)/shard_map/while
  211.3 6.1 %copy-start.18 = (f32[1,512]{1,0:T(1,128)S(1)}, f32[1,512]{1,0:T(1,128)}, u32[]{:S(2)}) copy-start(f32[1,512]{1,0:T(1,128)} %get-tuple-element.261) | copy-start | bytes 6148 | tf_op jit(solution)/shard_map/while
  211.3 6.1 %copy-start.19 = (f32[1,512]{1,0:T(1,128)S(1)}, f32[1,512]{1,0:T(1,128)}, u32[]{:S(2)}) copy-start(f32[1,512]{1,0:T(1,128)} %get-tuple-element.251) | copy-start | bytes 6148 | tf_op jit(solution)/shard_map/while
  211.3 6.1 %copy-start.20 = (f32[1,512]{1,0:T(1,128)S(1)}, f32[1,512]{1,0:T(1,128)}, u32[]{:S(2)}) copy-start(f32[1,512]{1,0:T(1,128)} %get-tuple-element.253) | copy-start | bytes 6148 | tf_op jit(solution)/shard_map/while
  211.3 6.1 %copy-start.21 = (f32[1,512]{1,0:T(1,128)S(1)}, f32[1,512]{1,0:T(1,128)}, u32[]{:S(2)}) copy-start(f32[1,512]{1,0:T(1,128)} %get-tuple-element.255) | copy-start | bytes 6148 | tf_op jit(solution)/shard_map/while
  214.0 2.5 %copy-start.4 = (f32[512,8,10]{0,1,2:T(8,128)S(1)}, f32[512,8,10]{0,1,2:T(8,128)}, u32[]{:S(2)}) copy-start(f32[512,8,10]{0,1,2:T(8,128)} %copy.154) | copy-start | bytes 491524 | tf_op jit(solution)/shard_map/while
  214.0 3.3 %copy-start.3 = (f32[512,8,10]{0,1,2:T(8,128)S(1)}, f32[512,8,10]{0,1,2:T(8,128)}, u32[]{:S(2)}) copy-start(f32[512,8,10]{0,1,2:T(8,128)} %copy.156) | copy-start | bytes 491524 | tf_op jit(solution)/shard_map/while
  214.0 3.3 %copy-start.5 = (f32[512,8,10]{0,1,2:T(8,128)S(1)}, f32[512,8,10]{0,1,2:T(8,128)}, u32[]{:S(2)}) copy-start(f32[512,8,10]{0,1,2:T(8,128)} %copy.155) | copy-start | bytes 491524 | tf_op jit(solution)/shard_map/while
  214.0 3.3 %copy-start.26 = (pred[512]{0:T(512)(128)(4,1)S(1)}, pred[512]{0:T(512)(128)(4,1)}, u32[]{:S(2)}) copy-start(pred[512]{0:T(512)(128)(4,1)} %compare_and_fusion.15) | copy-start | bytes 1540 | tf_op jit(solution)/shard_map/while
  214.0 3.4 %copy-start.2 = (f32[8,5,768]{2,0,1:T(8,128)S(1)}, f32[8,5,768]{2,0,1:T(8,128)}, u32[]{:S(2)}) copy-start(f32[8,5,768]{2,0,1:T(8,128)} %copy-done.1) | copy-start | bytes 368644 | tf_op jit(solution)/shard_map/while
  214.0 3.4 %copy-start.6 = (f32[8,10,512]{2,0,1:T(8,128)S(1)}, f32[8,10,512]{2,0,1:T(8,128)}, u32[]{:S(2)}) copy-start(f32[8,10,512]{2,0,1:T(8,128)} %get-tuple-element.260) | copy-start | bytes 491524 | tf_op jit(solution)/shard_map/while
  214.0 3.4 %copy-start.7 = (f32[8,10,512]{2,0,1:T(8,128)S(1)}, f32[8,10,512]{2,0,1:T(8,128)}, u32[]{:S(2)}) copy-start(f32[8,10,512]{2,0,1:T(8,128)} %get-tuple-element.249) | copy-start | bytes 491524 | tf_op jit(solution)/shard_map/while
  214.1 3.4 %copy-start.8 = (f32[8,10,512]{2,0,1:T(8,128)S(1)}, f32[8,10,512]{2,0,1:T(8,128)}, u32[]{:S(2)}) copy-start(f32[8,10,512]{2,0,1:T(8,128)} %get-tuple-element.258) | copy-start | bytes 491524 | tf_op jit(solution)/shard_map/while
  214.1 3.4 %copy-start.9 = (f32[8,10,512]{2,0,1:T(8,128)S(1)}, f32[8,10,512]{2,0,1:T(8,128)}, u32[]{:S(2)}) copy-start(f32[8,10,512]{2,0,1:T(8,128)} %get-tuple-element.247) | copy-start | bytes 491524 | tf_op jit(solution)/shard_map/while
  214.1 3.4 %copy-start.10 = (f32[8,10,512]{2,0,1:T(8,128)S(1)}, f32[8,10,512]{2,0,1:T(8,128)}, u32[]{:S(2)}) copy-start(f32[8,10,512]{2,0,1:T(8,128)} %get-tuple-element.256) | copy-start | bytes 491524 | tf_op jit(solution)/shard_map/while
  214.1 3.4 %copy-start.11 = (f32[8,10,512]{2,0,1:T(8,128)S(1)}, f32[8,10,512]{2,0,1:T(8,128)}, u32[]{:S(2)}) copy-start(f32[8,10,512]{2,0,1:T(8,128)} %get-tuple-element.245) | copy-start | bytes 491524 | tf_op jit(solution)/shard_map/while
  214.1 3.4 %copy-start.12 = (f32[8,10,512]{2,0,1:T(8,128)S(1)}, f32[8,10,512]{2,0,1:T(8,128)}, u32[]{:S(2)}) copy-start(f32[8,10,512]{2,0,1:T(8,128)} %get-tuple-element.254) | copy-start | bytes 491524 | tf_op jit(solution)/shard_map/while
  214.1 3.4 %copy-start.13 = (f32[8,10,512]{2,0,1:T(8,128)S(1)}, f32[8,10,512]{2,0,1:T(8,128)}, u32[]{:S(2)}) copy-start(f32[8,10,512]{2,0,1:T(8,128)} %get-tuple-element.243) | copy-start | bytes 491524 | tf_op jit(solution)/shard_map/while
  214.1 3.4 %copy-start.22 = (f32[1,512]{1,0:T(1,128)S(1)}, f32[1,512]{1,0:T(1,128)}, u32[]{:S(2)}) copy-start(f32[1,512]{1,0:T(1,128)} %get-tuple-element.257) | copy-start | bytes 6148 | tf_op jit(solution)/shard_map/while
  214.1 3.4 %copy-start.23 = (f32[1,512]{1,0:T(1,128)S(1)}, f32[1,512]{1,0:T(1,128)}, u32[]{:S(2)}) copy-start(f32[1,512]{1,0:T(1,128)} %get-tuple-element.259) | copy-start | bytes 6148 | tf_op jit(solution)/shard_map/while
  214.1 3.4 %copy-start.24 = (bf16[2,8,5,512]{3,1,2,0:T(8,128)(2,1)S(1)}, bf16[2,8,5,512]{3,1,2,0:T(8,128)(2,1)}, u32[]{:S(2)}) copy-start(bf16[2,8,5,512]{3,1,2,0:T(8,128)(2,1)} %get-tuple-element.272) | copy-start | bytes 245764 | tf_op jit(solution)/shard_map/while
  216.6 1.9 copy-start.16
  217.8 0.6 copy-start.25
where the time goes:
time: 232 us; the launch traced here: 230 us
  local copies, waits for them, and re-layouts  154 us (66%)
  other arithmetic  35.5 us (15%)
  blocking collectives  20.3 us (9%)
  starting transfers between devices  10.6 us (5%)
  waiting for transfers between devices  6.83 us (3%)
    gather x48, local copies, waits for them, and re-layouts, face_flux(): taken = jnp.take(stacked, neighbors[face_index], axis=2)  133 us
    select_n x24, other arithmetic, face_flux(): taken = jnp.take(stacked, neighbors[face_index], axis=2)  15.6 us
    psum x1, blocking collectives, local(): return lax.psum(closure_part, 'cell')  10.7 us
    ppermute x4, starting transfers between devices, from_behind(): return lax.ppermute(shard, axis, pairs)  10.6 us
    all_gather x1, blocking collectives, local(): whole_basis = lax.all_gather(basis, ('snap', 'var'), axis=0, tiled=True)  9.68 us
    concatenate x4, local copies, waits for them, and re-layouts, face_flux(): stacked = jnp.concatenate([extended, product], axis=1)  8.67 us
    ppermute x4, waiting for transfers between devices, from_behind(): return lax.ppermute(shard, axis, pairs)  6.83 us
    and x12, other arithmetic, face_flux(): taken = jnp.take(stacked, neighbors[face_index], axis=2)  6.67 us
  transfers between devices with their start and end apart: 4, of which 3 were waited for; matrix products, arithmetic and copies ran while one was open for 1% of the time, Pallas kernels for 0%

commit v1 on v0

--- a/solution.py
+++ b/solution.py
@@ -39,7 +39,23 @@
         return (jnp.take(field, send_lists[0], axis=2), jnp.take(field, send_lists[1], axis=2))
 
     true_to_prev, true_to_next = rim_rows(q_true)
-    whole_basis = lax.all_gather(basis, ("snap", "var"), axis=0, tiled=True)
+    xs = basis
+    n_now, piece_next, out_arr = (
+        lax.axis_size(("snap", "var")),
+        lax.axis_index(("snap", "var")),
+        xs.shape[0],
+    )
+    inbox = [b * n_now if dd == 0 else b for dd, b in enumerate(xs.shape)]
+    whole_basis = lax.dynamic_update_slice_in_dim(
+        jnp.zeros(inbox, xs.dtype), xs, piece_next * out_arr, axis=0
+    )
+    k0 = 1
+    while k0 < n_now:
+        xs = lax.ppermute(xs, ("snap", "var"), [(dd, (dd + 1) % n_now) for dd in range(n_now)])
+        whole_basis = lax.dynamic_update_slice_in_dim(
+            whole_basis, xs, (piece_next - k0) % n_now * out_arr, axis=0
+        )
+        k0 = k0 + 1
     basis_flat = whole_basis.reshape(whole_basis.shape[0], var_count * cell_count)
     rebuilt_sum = jnp.dot(coeffs, basis_flat, preferred_element_type=jnp.float32)
     rebuilt = rebuilt_sum.astype(jnp.bfloat16).reshape(snap_count, var_count, cell_count)

time: 232 us -> 253 us (1.091)
  local copies, waits for them, and re-layouts: 154 us -> 172 us
  waiting for transfers between devices: 6.83 us -> 17.4 us
  blocking collectives: 20.3 us -> 10.6 us
    dynamic_update_slice x0 -> x4, local copies, waits for them, and re-layouts: none -> 14.6 us  [the longest x3 12.5 us: local(): lax.dynamic_update_slice_in_dim(whole_basis, xs, (piece_next - k0) % n_no...]
    all_gather x1 -> x0, blocking collectives: 9.68 us -> none  [local(): whole_basis = lax.all_gather(basis, ('snap', 'var'), axis=0, tiled=True)]
    ppermute x0 -> x3, waiting for transfers between devices: none -> 9.08 us  [local(): lax.ppermute(xs, ('snap', 'var'), [(dd, (dd + 1) % n_now) for dd in range...]
  transfers between devices with their start and end apart: 4 -> 7, of which waited for: 3 -> 5; matrix products, arithmetic and copies ran while one was open for 1% -> 7% of each run, Pallas kernels for 0% -> 0%
where the time goes in v1:
time: 253 us; the launch traced here: 251 us
  local copies, waits for them, and re-layouts  172 us (68%)
  other arithmetic  36.2 us (14%)
  waiting for transfers between devices  17.4 us (7%)
  starting transfers between devices  12 us (5%)
  blocking collectives  10.6 us (4%)
    gather x48, local copies, waits for them, and re-layouts, face_flux(): taken = jnp.take(stacked, neighbors[face_index], axis=2)  134 us
    select_n x24, other arithmetic, face_flux(): taken = jnp.take(stacked, neighbors[face_index], axis=2)  15.4 us
    dynamic_update_slice x3, local copies, waits for them, and re-layouts, local(): lax.dynamic_update_slice_in_dim(whole_basis, xs, (piece_next - k0) % n_no...  12.5 us
    ppermute x4, starting transfers between devices, from_behind(): return lax.ppermute(shard, axis, pairs)  11.5 us
    psum x1, blocking collectives, local(): return lax.psum(closure_part, 'cell')  10.6 us
    ppermute x3, waiting for transfers between devices, local(): lax.ppermute(xs, ('snap', 'var'), [(dd, (dd + 1) % n_now) for dd in range...  9.08 us
    concatenate x4, local copies, waits for them, and re-layouts, face_flux(): stacked = jnp.concatenate([extended, product], axis=1)  8.67 us
    ppermute x4, waiting for transfers between devices, from_behind(): return lax.ppermute(shard, axis, pairs)  8.36 us
  transfers between devices with their start and end apart: 7, of which 5 were waited for; matrix products, arithmetic and copies ran while one was open for 7% of the time, Pallas kernels for 0%

profile of v1, /device:TPU:0, one launch (start us, length us, event | category | flops | bytes accessed | tf_op | source)
XLA Modules:
  0.0 251.1 jit_solution(8334772980485077125)
XLA Ops:
  0.5 5.1 %collective-permute-done.2 = bf16[32,5,512]{2,0,1:T(8,128)(2,1)S(1)} collective-permute-done((bf16[32,5,512]{2,0,1:T(8,128)(2,1)}, bf16[32,5,512]{2,0,1:T(8,128)(2,1)S(1)}, u32[]{:S(2)}, u32[]{:S(2)}) %collective-permute-start.2) | collective-permute-done | bytes 163872 | tf_op jit(solution)/shard_map/ppermute | solution.py:54
  6.4 3.9 %collective-permute-done.3 = bf16[32,5,512]{2,0,1:T(8,128)(2,1)S(1)} collective-permute-done((bf16[32,5,512]{2,0,1:T(8,128)(2,1)S(1)}, bf16[32,5,512]{2,0,1:T(8,128)(2,1)S(1)}, u32[]{:S(2)}, u32[]{:S(2)}) %collective-permute-start.3) | collective-permute-done | bytes 163872 | tf_op jit(solution)/shard_map/ppermute | solution.py:54
  14.8 2.1 dynamic_update_slice.16
  17.3 4.2 %dynamic_update_slice.17 = bf16[128,5,512]{0,2,1:T(8,128)(2,1)S(1)} dynamic-update-slice(bf16[128,5,512]{0,2,1:T(8,128)(2,1)S(1)} %dynamic_update_slice.16, bf16[32,5,512]{0,2,1:T(8,128)(2,1)S(1)} %copy.133, s32[]{:T(128)S(6)} %select_n.43, s32[]{:T(128)} %copy.189, s32[]{:T(128)} %copy.189) | dynamic-update-slice | bytes 327684 | tf_op jit(solution)/shard_map/dynamic_update_slice | solution.py:55
  21.8 4.2 %dynamic_update_slice.18 = bf16[128,5,512]{0,2,1:T(8,128)(2,1)S(1)} dynamic-update-slice(bf16[128,5,512]{0,2,1:T(8,128)(2,1)S(1)} %dynamic_update_slice.17, bf16[32,5,512]{0,2,1:T(8,128)(2,1)S(1)} %copy.134, s32[]{:T(128)S(6)} %select_n.45, s32[]{:T(128)} %copy.189, s32[]{:T(128)} %copy.189) | dynamic-update-slice | bytes 327684 | tf_op jit(solution)/shard_map/dynamic_update_slice | solution.py:55
  26.3 4.2 %dynamic_update_slice.19 = bf16[128,5,512]{0,2,1:T(8,128)(2,1)S(1)} dynamic-update-slice(bf16[128,5,512]{0,2,1:T(8,128)(2,1)S(1)} %dynamic_update_slice.18, bf16[32,5,512]{0,2,1:T(8,128)(2,1)S(1)} %copy.135, s32[]{:T(128)S(6)} %select_n.47, s32[]{:T(128)} %copy.189, s32[]{:T(128)} %copy.189) | dynamic-update-slice | bytes 327684 | tf_op jit(solution)/shard_map/dynamic_update_slice | solution.py:55
  33.3 4.3 %collective-permute-start = (bf16[16,5,128]{0,1,2:T(8,128)(2,1)S(1)}, bf16[16,5,128]{0,1,2:T(8,128)(2,1)S(1)}, u32[]{:S(2)}, u32[]{:S(2)}) collective-permute-start(bf16[16,5,128]{0,1,2:T(8,128)(2,1)S(1)} %get-tuple-element.158), channel_id=1, source_target_pairs={{0,4},{4,8},{8,12},{1,5},{5,9},{9,13},{2,6},{6,10},{10,14},{3,7},{... | collective-permute-start | bytes 61448 | tf_op jit(solution)/shard_map/ppermute | solution.py:13
  39.8 4.6 %collective-permute-start.5 = (bf16[16,5,128]{0,1,2:T(8,128)(2,1)S(1)}, bf16[16,5,128]{0,1,2:T(8,128)(2,1)S(1)}, u32[]{:S(2)}, u32[]{:S(2)}) collective-permute-start(bf16[16,5,128]{0,1,2:T(8,128)(2,1)S(1)} %get-tuple-element.157), channel_id=1, source_target_pairs={{0,4},{4,8},{8,12},{1,5},{5,9},{9,13},{2,6},{6,10},{10,14},{3,7},{... | collective-permute-start | bytes 61448 | tf_op jit(solution)/shard_map/ppermute | solution.py:13
  45.8 2.8 %collective-permute-done.1 = bf16[16,5,128]{0,1,2:T(8,128)(2,1)S(1)} collective-permute-done((bf16[16,5,128]{0,1,2:T(8,128)(2,1)S(1)}, bf16[16,5,128]{0,1,2:T(8,128)(2,1)S(1)}, u32[]{:S(2)}, u32[]{:S(2)}) %collective-permute-start.1) | collective-permute-done | bytes 20512 | tf_op jit(solution)/shard_map/ppermute | solution.py:13
  51.2 4.0 %collective-permute-done.6 = bf16[16,5,128]{0,1,2:T(8,128)(2,1)S(1)} collective-permute-done((bf16[16,5,128]{0,1,2:T(8,128)(2,1)S(1)}, bf16[16,5,128]{0,1,2:T(8,128)(2,1)S(1)}, u32[]{:S(2)}, u32[]{:S(2)}) %collective-permute-start.6) | collective-permute-done | bytes 20512 | tf_op jit(solution)/shard_map/ppermute | solution.py:13
  56.0 183.2 %while.11 = (s32[]{:T(128)}, bf16[2,8,5,512]{3,1,2,0:T(8,128)(2,1)}, f32[5,512]{1,0:T(8,128)}, f32[6,512]{1,0:T(8,128)}, bf16[2,8,5,768]{3,1,0,2:T(8,128)(2,1)},...) while((s32[]{:T(128)}, bf16[2,8,5,512]{3,1,2,0:T(8,128)(2,1)}, ...), condition=%wide.region_1.4_spmd.clone, body=%wide.region_0.3_spmd.clone.sunk | while | flops 2576898 | bytes 26092312 | solution.py:82
  67.4 2.2 copy.164
  69.6 2.8 %gather_fusion.11 = f32[512,8,10]{2,1,0:T(8,128)} fusion(f32[8,10,768]{1,0,2:T(8,128)S(1)} %copy.164, s32[1024]{0:T(1024)} %pad_clamp_fusion.19), kind=kCustom, calls=%fused_computation.10.clone.clone.1 | custom fusion | bytes 329728 | tf_op jit(solution)/shard_map/while/body/eval_jaxpr/jit(_take)/gather | solution.py:25
  72.4 2.9 %copy.175 = f32[512,8,10]{0,1,2:T(8,128)} copy(f32[512,8,10]{2,1,0:T(8,128)} %gather_fusion.11) | data formatting | bytes 327680 | tf_op jit(solution)/shard_map/while/body/eval_jaxpr/jit(_take)/gather | solution.py:25
  75.3 2.7 %gather_fusion.9 = f32[512,8,10]{2,1,0:T(8,128)} fusion(f32[8,10,768]{1,0,2:T(8,128)S(1)} %copy.164, s32[1024]{0:T(1024)S(1)} %pad_clamp_fusion.18), kind=kCustom, calls=%fused_computation.11.clone.clone.1 | custom fusion | bytes 329728 | tf_op jit(solution)/shard_map/while/body/eval_jaxpr/jit(_take)/gather | solution.py:25
  78.0 2.9 %copy.173 = f32[512,8,10]{0,1,2:T(8,128)} copy(f32[512,8,10]{2,1,0:T(8,128)} %gather_fusion.9) | data formatting | bytes 327680 | tf_op jit(solution)/shard_map/while/body/eval_jaxpr/jit(_take)/gather | solution.py:25
  80.9 2.7 %gather_fusion.7 = f32[512,8,10]{2,1,0:T(8,128)} fusion(f32[8,10,768]{1,0,2:T(8,128)S(1)} %copy.164, s32[1024]{0:T(1024)S(1)} %pad_clamp_fusion.17), kind=kCustom, calls=%fused_computation.12.clone.clone.1 | custom fusion | bytes 329728 | tf_op jit(solution)/shard_map/while/body/eval_jaxpr/jit(_take)/gather | solution.py:25
  83.6 2.9 %copy.171 = f32[512,8,10]{0,1,2:T(8,128)} copy(f32[512,8,10]{2,1,0:T(8,128)} %gather_fusion.7) | data formatting | bytes 327680 | tf_op jit(solution)/shard_map/while/body/eval_jaxpr/jit(_take)/gather | solution.py:25
  86.4 2.7 %gather_fusion.5 = f32[512,8,10]{2,1,0:T(8,128)} fusion(f32[8,10,768]{1,0,2:T(8,128)S(1)} %copy.164, s32[1024]{0:T(1024)S(1)} %pad_clamp_fusion.16), kind=kCustom, calls=%fused_computation.13.clone.clone.1 | custom fusion | bytes 329728 | tf_op jit(solution)/shard_map/while/body/eval_jaxpr/jit(_take)/gather | solution.py:25
  89.1 2.9 %copy.169 = f32[512,8,10]{0,1,2:T(8,128)} copy(f32[512,8,10]{2,1,0:T(8,128)} %gather_fusion.5) | data formatting | bytes 327680 | tf_op jit(solution)/shard_map/while/body/eval_jaxpr/jit(_take)/gather | solution.py:25
  92.0 2.7 %gather_fusion.3 = f32[512,8,10]{2,1,0:T(8,128)} fusion(f32[8,10,768]{1,0,2:T(8,128)S(1)} %copy.164, s32[1024]{0:T(1024)S(1)} %pad_clamp_fusion.15), kind=kCustom, calls=%fused_computation.14.clone.clone.1 | custom fusion | bytes 329728 | tf_op jit(solution)/shard_map/while/body/eval_jaxpr/jit(_take)/gather | solution.py:25
  94.7 2.9 %copy.167 = f32[512,8,10]{0,1,2:T(8,128)} copy(f32[512,8,10]{2,1,0:T(8,128)} %gather_fusion.3) | data formatting | bytes 327680 | tf_op jit(solution)/shard_map/while/body/eval_jaxpr/jit(_take)/gather | solution.py:25
  97.6 2.7 %gather_fusion.1 = f32[512,8,10]{2,1,0:T(8,128)} fusion(f32[8,10,768]{1,0,2:T(8,128)S(1)} %copy.164, s32[1024]{0:T(1024)S(1)} %pad_clamp_fusion.14), kind=kCustom, calls=%fused_computation.15.clone.clone.1 | custom fusion | bytes 329728 | tf_op jit(solution)/shard_map/while/body/eval_jaxpr/jit(_take)/gather | solution.py:25
  100.3 2.9 %copy.165 = f32[512,8,10]{0,1,2:T(8,128)} copy(f32[512,8,10]{2,1,0:T(8,128)} %gather_fusion.1) | data formatting | bytes 327680 | tf_op jit(solution)/shard_map/while/body/eval_jaxpr/jit(_take)/gather | solution.py:25
  103.2 2.2 copy.162
  105.3 2.8 %gather_fusion.10 = f32[512,8,10]{2,1,0:T(8,128)} fusion(f32[8,10,768]{1,0,2:T(8,128)S(1)} %copy.162, s32[1024]{0:T(1024)} %pad_clamp_fusion.19), kind=kCustom, calls=%fused_computation.1.clone.clone.1 | custom fusion | bytes 329728 | tf_op jit(solution)/shard_map/while/body/eval_jaxpr/jit(_take)/gather | solution.py:25
  108.2 2.9 %copy.174 = f32[512,8,10]{0,1,2:T(8,128)} copy(f32[512,8,10]{2,1,0:T(8,128)} %gather_fusion.10) | data formatting | bytes 327680 | tf_op jit(solution)/shard_map/while/body/eval_jaxpr/jit(_take)/gather | solution.py:25
  112.8 2.7 %gather_fusion.8 = f32[512,8,10]{2,1,0:T(8,128)} fusion(f32[8,10,768]{1,0,2:T(8,128)S(1)} %copy.162, s32[1024]{0:T(1024)S(1)} %pad_clamp_fusion.18), kind=kCustom, calls=%fused_computation.5.clone.clone.1 | custom fusion | bytes 329728 | tf_op jit(solution)/shard_map/while/body/eval_jaxpr/jit(_take)/gather | solution.py:25
  115.5 2.9 %copy.172 = f32[512,8,10]{0,1,2:T(8,128)} copy(f32[512,8,10]{2,1,0:T(8,128)} %gather_fusion.8) | data formatting | bytes 327680 | tf_op jit(solution)/shard_map/while/body/eval_jaxpr/jit(_take)/gather | solution.py:25
  120.1 2.7 %gather_fusion.6 = f32[512,8,10]{2,1,0:T(8,128)} fusion(f32[8,10,768]{1,0,2:T(8,128)S(1)} %copy.162, s32[1024]{0:T(1024)S(1)} %pad_clamp_fusion.17), kind=kCustom, calls=%fused_computation.6.clone.clone.1 | custom fusion | bytes 329728 | tf_op jit(solution)/shard_map/while/body/eval_jaxpr/jit(_take)/gather | solution.py:25
  122.8 2.9 %copy.170 = f32[512,8,10]{0,1,2:T(8,128)} copy(f32[512,8,10]{2,1,0:T(8,128)} %gather_fusion.6) | data formatting | bytes 327680 | tf_op jit(solution)/shard_map/while/body/eval_jaxpr/jit(_take)/gather | solution.py:25
  127.5 2.7 %gather_fusion.4 = f32[512,8,10]{2,1,0:T(8,128)} fusion(f32[8,10,768]{1,0,2:T(8,128)S(1)} %copy.162, s32[1024]{0:T(1024)S(1)} %pad_clamp_fusion.16), kind=kCustom, calls=%fused_computation.7.clone.clone.1 | custom fusion | bytes 329728 | tf_op jit(solution)/shard_map/while/body/eval_jaxpr/jit(_take)/gather | solution.py:25
  130.2 2.9 %copy.168 = f32[512,8,10]{0,1,2:T(8,128)} copy(f32[512,8,10]{2,1,0:T(8,128)} %gather_fusion.4) | data formatting | bytes 327680 | tf_op jit(solution)/shard_map/while/body/eval_jaxpr/jit(_take)/gather | solution.py:25
  134.9 2.7 %gather_fusion.2 = f32[512,8,10]{2,1,0:T(8,128)} fusion(f32[8,10,768]{1,0,2:T(8,128)S(1)} %copy.162, s32[1024]{0:T(1024)S(1)} %pad_clamp_fusion.15), kind=kCustom, calls=%fused_computation.8.clone.clone.1 | custom fusion | bytes 329728 | tf_op jit(solution)/shard_map/while/body/eval_jaxpr/jit(_take)/gather | solution.py:25
  137.6 2.9 %copy.166 = f32[512,8,10]{0,1,2:T(8,128)} copy(f32[512,8,10]{2,1,0:T(8,128)} %gather_fusion.2) | data formatting | bytes 327680 | tf_op jit(solution)/shard_map/while/body/eval_jaxpr/jit(_take)/gather | solution.py:25
  140.5 2.7 %gather_fusion = f32[512,8,10]{2,1,0:T(8,128)} fusion(f32[8,10,768]{1,0,2:T(8,128)S(1)} %copy.162, s32[1024]{0:T(1024)S(1)} %pad_clamp_fusion.14), kind=kCustom, calls=%fused_computation.9.clone.clone.1 | custom fusion | bytes 329728 | tf_op jit(solution)/shard_map/while/body/eval_jaxpr/jit(_take)/gather | solution.py:25
  143.3 2.4 copy.163
  159.0 2.2 copy.164
  161.2 2.8 %gather_fusion.11 = f32[512,8,10]{2,1,0:T(8,128)} fusion(f32[8,10,768]{1,0,2:T(8,128)S(1)} %copy.164, s32[1024]{0:T(1024)} %pad_clamp_fusion.19), kind=kCustom, calls=%fused_computation.10.clone.clone.1 | custom fusion | bytes 329728 | tf_op jit(solution)/shard_map/while/body/eval_jaxpr/jit(_take)/gather | solution.py:25
  164.0 2.9 %copy.175 = f32[512,8,10]{0,1,2:T(8,128)} copy(f32[512,8,10]{2,1,0:T(8,128)} %gather_fusion.11) | data formatting | bytes 327680 | tf_op jit(solution)/shard_map/while/body/eval_jaxpr/jit(_take)/gather | solution.py:25
  166.9 2.7 %gather_fusion.9 = f32[512,8,10]{2,1,0:T(8,128)} fusion(f32[8,10,768]{1,0,2:T(8,128)S(1)} %copy.164, s32[1024]{0:T(1024)S(1)} %pad_clamp_fusion.18), kind=kCustom, calls=%fused_computation.11.clone.clone.1 | custom fusion | bytes 329728 | tf_op jit(solution)/shard_map/while/body/eval_jaxpr/jit(_take)/gather | solution.py:25
  169.6 2.9 %copy.173 = f32[512,8,10]{0,1,2:T(8,128)} copy(f32[512,8,10]{2,1,0:T(8,128)} %gather_fusion.9) | data formatting | bytes 327680 | tf_op jit(solution)/shard_map/while/body/eval_jaxpr/jit(_take)/gather | solution.py:25
  172.4 2.7 %gather_fusion.7 = f32[512,8,10]{2,1,0:T(8,128)} fusion(f32[8,10,768]{1,0,2:T(8,128)S(1)} %copy.164, s32[1024]{0:T(1024)S(1)} %pad_clamp_fusion.17), kind=kCustom, calls=%fused_computation.12.clone.clone.1 | custom fusion | bytes 329728 | tf_op jit(solution)/shard_map/while/body/eval_jaxpr/jit(_take)/gather | solution.py:25
  175.1 2.9 %copy.171 = f32[512,8,10]{0,1,2:T(8,128)} copy(f32[512,8,10]{2,1,0:T(8,128)} %gather_fusion.7) | data formatting | bytes 327680 | tf_op jit(solution)/shard_map/while/body/eval_jaxpr/jit(_take)/gather | solution.py:25
  178.0 2.7 %gather_fusion.5 = f32[512,8,10]{2,1,0:T(8,128)} fusion(f32[8,10,768]{1,0,2:T(8,128)S(1)} %copy.164, s32[1024]{0:T(1024)S(1)} %pad_clamp_fusion.16), kind=kCustom, calls=%fused_computation.13.clone.clone.1 | custom fusion | bytes 329728 | tf_op jit(solution)/shard_map/while/body/eval_jaxpr/jit(_take)/gather | solution.py:25
  180.7 2.9 %copy.169 = f32[512,8,10]{0,1,2:T(8,128)} copy(f32[512,8,10]{2,1,0:T(8,128)} %gather_fusion.5) | data formatting | bytes 327680 | tf_op jit(solution)/shard_map/while/body/eval_jaxpr/jit(_take)/gather | solution.py:25
  183.6 2.7 %gather_fusion.3 = f32[512,8,10]{2,1,0:T(8,128)} fusion(f32[8,10,768]{1,0,2:T(8,128)S(1)} %copy.164, s32[1024]{0:T(1024)S(1)} %pad_clamp_fusion.15), kind=kCustom, calls=%fused_computation.14.clone.clone.1 | custom fusion | bytes 329728 | tf_op jit(solution)/shard_map/while/body/eval_jaxpr/jit(_take)/gather | solution.py:25
  186.3 2.9 %copy.167 = f32[512,8,10]{0,1,2:T(8,128)} copy(f32[512,8,10]{2,1,0:T(8,128)} %gather_fusion.3) | data formatting | bytes 327680 | tf_op jit(solution)/shard_map/while/body/eval_jaxpr/jit(_take)/gather | solution.py:25
  189.2 2.7 %gather_fusion.1 = f32[512,8,10]{2,1,0:T(8,128)} fusion(f32[8,10,768]{1,0,2:T(8,128)S(1)} %copy.164, s32[1024]{0:T(1024)S(1)} %pad_clamp_fusion.14), kind=kCustom, calls=%fused_computation.15.clone.clone.1 | custom fusion | bytes 329728 | tf_op jit(solution)/shard_map/while/body/eval_jaxpr/jit(_take)/gather | solution.py:25
  191.9 2.9 %copy.165 = f32[512,8,10]{0,1,2:T(8,128)} copy(f32[512,8,10]{2,1,0:T(8,128)} %gather_fusion.1) | data formatting | bytes 327680 | tf_op jit(solution)/shard_map/while/body/eval_jaxpr/jit(_take)/gather | solution.py:25
  194.7 2.2 copy.162
  196.9 2.8 %gather_fusion.10 = f32[512,8,10]{2,1,0:T(8,128)} fusion(f32[8,10,768]{1,0,2:T(8,128)S(1)} %copy.162, s32[1024]{0:T(1024)} %pad_clamp_fusion.19), kind=kCustom, calls=%fused_computation.1.clone.clone.1 | custom fusion | bytes 329728 | tf_op jit(solution)/shard_map/while/body/eval_jaxpr/jit(_take)/gather | solution.py:25
  199.7 2.9 %copy.174 = f32[512,8,10]{0,1,2:T(8,128)} copy(f32[512,8,10]{2,1,0:T(8,128)} %gather_fusion.10) | data formatting | bytes 327680 | tf_op jit(solution)/shard_map/while/body/eval_jaxpr/jit(_take)/gather | solution.py:25
  204.4 2.7 %gather_fusion.8 = f32[512,8,10]{2,1,0:T(8,128)} fusion(f32[8,10,768]{1,0,2:T(8,128)S(1)} %copy.162, s32[1024]{0:T(1024)S(1)} %pad_clamp_fusion.18), kind=kCustom, calls=%fused_computation.5.clone.clone.1 | custom fusion | bytes 329728 | tf_op jit(solution)/shard_map/while/body/eval_jaxpr/jit(_take)/gather | solution.py:25
  207.1 2.9 %copy.172 = f32[512,8,10]{0,1,2:T(8,128)} copy(f32[512,8,10]{2,1,0:T(8,128)} %gather_fusion.8) | data formatting | bytes 327680 | tf_op jit(solution)/shard_map/while/body/eval_jaxpr/jit(_take)/gather | solution.py:25
  211.7 2.7 %gather_fusion.6 = f32[512,8,10]{2,1,0:T(8,128)} fusion(f32[8,10,768]{1,0,2:T(8,128)S(1)} %copy.162, s32[1024]{0:T(1024)S(1)} %pad_clamp_fusion.17), kind=kCustom, calls=%fused_computation.6.clone.clone.1 | custom fusion | bytes 329728 | tf_op jit(solution)/shard_map/while/body/eval_jaxpr/jit(_take)/gather | solution.py:25
  214.4 2.9 %copy.170 = f32[512,8,10]{0,1,2:T(8,128)} copy(f32[512,8,10]{2,1,0:T(8,128)} %gather_fusion.6) | data formatting | bytes 327680 | tf_op jit(solution)/shard_map/while/body/eval_jaxpr/jit(_take)/gather | solution.py:25
  219.1 2.7 %gather_fusion.4 = f32[512,8,10]{2,1,0:T(8,128)} fusion(f32[8,10,768]{1,0,2:T(8,128)S(1)} %copy.162, s32[1024]{0:T(1024)S(1)} %pad_clamp_fusion.16), kind=kCustom, calls=%fused_computation.7.clone.clone.1 | custom fusion | bytes 329728 | tf_op jit(solution)/shard_map/while/body/eval_jaxpr/jit(_take)/gather | solution.py:25
  221.8 2.9 %copy.168 = f32[512,8,10]{0,1,2:T(8,128)} copy(f32[512,8,10]{2,1,0:T(8,128)} %gather_fusion.4) | data formatting | bytes 327680 | tf_op jit(solution)/shard_map/while/body/eval_jaxpr/jit(_take)/gather | solution.py:25
  226.4 2.7 %gather_fusion.2 = f32[512,8,10]{2,1,0:T(8,128)} fusion(f32[8,10,768]{1,0,2:T(8,128)S(1)} %copy.162, s32[1024]{0:T(1024)S(1)} %pad_clamp_fusion.15), kind=kCustom, calls=%fused_computation.8.clone.clone.1 | custom fusion | bytes 329728 | tf_op jit(solution)/shard_map/while/body/eval_jaxpr/jit(_take)/gather | solution.py:25
  229.2 2.9 %copy.166 = f32[512,8,10]{0,1,2:T(8,128)} copy(f32[512,8,10]{2,1,0:T(8,128)} %gather_fusion.2) | data formatting | bytes 327680 | tf_op jit(solution)/shard_map/while/body/eval_jaxpr/jit(_take)/gather | solution.py:25
  232.1 2.7 %gather_fusion = f32[512,8,10]{2,1,0:T(8,128)} fusion(f32[8,10,768]{1,0,2:T(8,128)S(1)} %copy.162, s32[1024]{0:T(1024)S(1)} %pad_clamp_fusion.14), kind=kCustom, calls=%fused_computation.9.clone.clone.1 | custom fusion | bytes 329728 | tf_op jit(solution)/shard_map/while/body/eval_jaxpr/jit(_take)/gather | solution.py:25
  234.9 2.4 copy.163
  240.4 10.6 %psum.7 = f32[16,128]{1,0:T(8,128)} all-reduce(f32[16,128]{1,0:T(8,128)S(1)} %fusion.66), channel_id=1, replica_groups=mesh['grp'=2,'cell'=4,'snap'=2,'var'=2] {'cell'}, use_global_device_ids=true, to_apply=%region_2.5 | all-reduce | flops 2048 | bytes 16384 | tf_op jit(solution)/shard_map/psum | solution.py:88
  (208 shorter events, 57.1 us)
Async XLA Ops:
  0.0 30.5 %copy-start = (bf16[16,128]{1,0:T(8,128)(2,1)S(1)}, bf16[16,128]{1,0:T(8,128)(2,1)}, u32[]{:S(2)}) copy-start(bf16[16,128]{1,0:T(8,128)(2,1)} %param.15) | copy-start | bytes 12292
  0.0 5.6 %collective-permute-start.2 = (bf16[32,5,512]{2,0,1:T(8,128)(2,1)}, bf16[32,5,512]{2,0,1:T(8,128)(2,1)S(1)}, u32[]{:S(2)}, u32[]{:S(2)}) collective-permute-start(bf16[32,5,512]{2,0,1:T(8,128)(2,1)} %param.16), channel_id=1, source_target_pairs={{0,1},{1,2},{2,3},{3,0},{4,5},{5,6},{6,7},{7,4},{8,9},{9,10},{10,1... | collective-permute-start | bytes 491528 | tf_op jit(solution)/shard_map/ppermute | solution.py:54
  5.6 4.7 %collective-permute-start.3 = (bf16[32,5,512]{2,0,1:T(8,128)(2,1)S(1)}, bf16[32,5,512]{2,0,1:T(8,128)(2,1)S(1)}, u32[]{:S(2)}, u32[]{:S(2)}) collective-permute-start(bf16[32,5,512]{2,0,1:T(8,128)(2,1)S(1)} %collective-permute-done.2), channel_id=1, source_target_pairs={{0,1},{1,2},{2,3},{3,0},{4,5},{5,6},{6,7},{7,4},{8,9},{9,10},{10,1... | collective-permute-start | bytes 491528 | tf_op jit(solution)/shard_map/ppermute | solution.py:54
  10.3 15.6 %collective-permute-start.4 = (bf16[32,5,512]{2,0,1:T(8,128)(2,1)S(1)}, bf16[32,5,512]{2,0,1:T(8,128)(2,1)S(1)}, u32[]{:S(2)}, u32[]{:S(2)}) collective-permute-start(bf16[32,5,512]{2,0,1:T(8,128)(2,1)S(1)} %collective-permute-done.3), channel_id=1, source_target_pairs={{0,1},{1,2},{2,3},{3,0},{4,5},{5,6},{6,7},{7,4},{8,9},{9,10},{10,1... | collective-permute-start | bytes 491528 | tf_op jit(solution)/shard_map/ppermute | solution.py:54
  30.5 7.4 %copy-start.14 = (bf16[128,5,512]{0,2,1:T(8,128)(2,1)}, bf16[128,5,512]{0,2,1:T(8,128)(2,1)S(1)}, u32[]{:S(2)}) copy-start(bf16[128,5,512]{0,2,1:T(8,128)(2,1)S(1)} %dynamic_update_slice.19) | copy-start | bytes 1966084
  30.7 18.0 %copy-start.15 = (bf16[16,5,512]{2,0,1:T(8,128)(2,1)S(1)}, bf16[16,5,512]{2,0,1:T(8,128)(2,1)}, u32[]{:S(2)}) copy-start(bf16[16,5,512]{2,0,1:T(8,128)(2,1)} %param.14) | copy-start | bytes 245764
  33.3 12.4 %collective-permute-start = (bf16[16,5,128]{0,1,2:T(8,128)(2,1)S(1)}, bf16[16,5,128]{0,1,2:T(8,128)(2,1)S(1)}, u32[]{:S(2)}, u32[]{:S(2)}) collective-permute-start(bf16[16,5,128]{0,1,2:T(8,128)(2,1)S(1)} %get-tuple-element.158), channel_id=1, source_target_pairs={{0,4},{4,8},{8,12},{1,5},{5,9},{9,13},{2,6},{6,10},{10,14},{3,7},{... | collective-permute-start | bytes 61448 | tf_op jit(solution)/shard_map/ppermute | solution.py:13
  37.8 10.8 %collective-permute-start.1 = (bf16[16,5,128]{0,1,2:T(8,128)(2,1)S(1)}, bf16[16,5,128]{0,1,2:T(8,128)(2,1)S(1)}, u32[]{:S(2)}, u32[]{:S(2)}) collective-permute-start(bf16[16,5,128]{0,1,2:T(8,128)(2,1)S(1)} %get-tuple-element.160), channel_id=1, source_target_pairs={{4,0},{8,4},{12,8},{5,1},{9,5},{13,9},{6,2},{10,6},{14,10},{7,3},{... | collective-permute-start | bytes 61448 | tf_op jit(solution)/shard_map/ppermute | solution.py:13
  39.8 11.2 %collective-permute-start.5 = (bf16[16,5,128]{0,1,2:T(8,128)(2,1)S(1)}, bf16[16,5,128]{0,1,2:T(8,128)(2,1)S(1)}, u32[]{:S(2)}, u32[]{:S(2)}) collective-permute-start(bf16[16,5,128]{0,1,2:T(8,128)(2,1)S(1)} %get-tuple-element.157), channel_id=1, source_target_pairs={{0,4},{4,8},{8,12},{1,5},{5,9},{9,13},{2,6},{6,10},{10,14},{3,7},{... | collective-permute-start | bytes 61448 | tf_op jit(solution)/shard_map/ppermute | solution.py:13
  44.3 10.8 %collective-permute-start.6 = (bf16[16,5,128]{0,1,2:T(8,128)(2,1)S(1)}, bf16[16,5,128]{0,1,2:T(8,128)(2,1)S(1)}, u32[]{:S(2)}, u32[]{:S(2)}) collective-permute-start(bf16[16,5,128]{0,1,2:T(8,128)(2,1)S(1)} %get-tuple-element.159), channel_id=1, source_target_pairs={{4,0},{8,4},{12,8},{5,1},{9,5},{13,9},{6,2},{10,6},{14,10},{7,3},{... | collective-permute-start | bytes 61448 | tf_op jit(solution)/shard_map/ppermute | solution.py:13
  65.9 0.7 copy-start.1
  118.4 7.4 %copy-start.26 = (pred[512]{0:T(512)(128)(4,1)S(1)}, pred[512]{0:T(512)(128)(4,1)}, u32[]{:S(2)}) copy-start(pred[512]{0:T(512)(128)(4,1)} %compare_and_fusion.17) | copy-start | bytes 1540 | tf_op jit(solution)/shard_map/while
  125.7 7.4 %copy-start.25 = (pred[512]{0:T(512)(128)(4,1)S(1)}, pred[512]{0:T(512)(128)(4,1)}, u32[]{:S(2)}) copy-start(pred[512]{0:T(512)(128)(4,1)} %compare_and_fusion.16) | copy-start | bytes 1540 | tf_op jit(solution)/shard_map/while
  140.5 6.0 %copy-start.16 = (f32[1,512]{1,0:T(1,128)S(1)}, f32[1,512]{1,0:T(1,128)}, u32[]{:S(2)}) copy-start(f32[1,512]{1,0:T(1,128)} %get-tuple-element.261) | copy-start | bytes 6148 | tf_op jit(solution)/shard_map/while
  140.5 6.0 %copy-start.17 = (f32[1,512]{1,0:T(1,128)S(1)}, f32[1,512]{1,0:T(1,128)}, u32[]{:S(2)}) copy-start(f32[1,512]{1,0:T(1,128)} %get-tuple-element.251) | copy-start | bytes 6148 | tf_op jit(solution)/shard_map/while
  140.5 6.0 %copy-start.18 = (f32[1,512]{1,0:T(1,128)S(1)}, f32[1,512]{1,0:T(1,128)}, u32[]{:S(2)}) copy-start(f32[1,512]{1,0:T(1,128)} %get-tuple-element.253) | copy-start | bytes 6148 | tf_op jit(solution)/shard_map/while
  140.5 6.0 %copy-start.19 = (f32[1,512]{1,0:T(1,128)S(1)}, f32[1,512]{1,0:T(1,128)}, u32[]{:S(2)}) copy-start(f32[1,512]{1,0:T(1,128)} %get-tuple-element.255) | copy-start | bytes 6148 | tf_op jit(solution)/shard_map/while
  143.2 2.5 %copy-start.4 = (f32[512,8,10]{0,1,2:T(8,128)S(1)}, f32[512,8,10]{0,1,2:T(8,128)}, u32[]{:S(2)}) copy-start(f32[512,8,10]{0,1,2:T(8,128)} %copy.165) | copy-start | bytes 491524 | tf_op jit(solution)/shard_map/while
  143.2 3.2 %copy-start.3 = (f32[512,8,10]{0,1,2:T(8,128)S(1)}, f32[512,8,10]{0,1,2:T(8,128)}, u32[]{:S(2)}) copy-start(f32[512,8,10]{0,1,2:T(8,128)} %copy.167) | copy-start | bytes 491524 | tf_op jit(solution)/shard_map/while
  143.2 3.2 %copy-start.5 = (f32[512,8,10]{0,1,2:T(8,128)S(1)}, f32[512,8,10]{0,1,2:T(8,128)}, u32[]{:S(2)}) copy-start(f32[512,8,10]{0,1,2:T(8,128)} %copy.166) | copy-start | bytes 491524 | tf_op jit(solution)/shard_map/while
  143.2 3.2 %copy-start.24 = (pred[512]{0:T(512)(128)(4,1)S(1)}, pred[512]{0:T(512)(128)(4,1)}, u32[]{:S(2)}) copy-start(pred[512]{0:T(512)(128)(4,1)} %compare_and_fusion.15) | copy-start | bytes 1540 | tf_op jit(solution)/shard_map/while
  143.2 3.3 %copy-start.2 = (f32[8,5,768]{2,0,1:T(8,128)S(1)}, f32[8,5,768]{2,0,1:T(8,128)}, u32[]{:S(2)}) copy-start(f32[8,5,768]{2,0,1:T(8,128)} %copy-done.1) | copy-start | bytes 368644 | tf_op jit(solution)/shard_map/while
  143.2 3.3 %copy-start.6 = (f32[8,10,512]{2,0,1:T(8,128)S(1)}, f32[8,10,512]{2,0,1:T(8,128)}, u32[]{:S(2)}) copy-start(f32[8,10,512]{2,0,1:T(8,128)} %get-tuple-element.260) | copy-start | bytes 491524 | tf_op jit(solution)/shard_map/while
  143.2 3.3 %copy-start.7 = (f32[8,10,512]{2,0,1:T(8,128)S(1)}, f32[8,10,512]{2,0,1:T(8,128)}, u32[]{:S(2)}) copy-start(f32[8,10,512]{2,0,1:T(8,128)} %get-tuple-element.249) | copy-start | bytes 491524 | tf_op jit(solution)/shard_map/while
  143.2 3.3 %copy-start.8 = (f32[8,10,512]{2,0,1:T(8,128)S(1)}, f32[8,10,512]{2,0,1:T(8,128)}, u32[]{:S(2)}) copy-start(f32[8,10,512]{2,0,1:T(8,128)} %get-tuple-element.258) | copy-start | bytes 491524 | tf_op jit(solution)/shard_map/while
  143.2 3.3 %copy-start.9 = (f32[8,10,512]{2,0,1:T(8,128)S(1)}, f32[8,10,512]{2,0,1:T(8,128)}, u32[]{:S(2)}) copy-start(f32[8,10,512]{2,0,1:T(8,128)} %get-tuple-element.247) | copy-start | bytes 491524 | tf_op jit(solution)/shard_map/while
  143.3 3.3 %copy-start.10 = (f32[8,10,512]{2,0,1:T(8,128)S(1)}, f32[8,10,512]{2,0,1:T(8,128)}, u32[]{:S(2)}) copy-start(f32[8,10,512]{2,0,1:T(8,128)} %get-tuple-element.256) | copy-start | bytes 491524 | tf_op jit(solution)/shard_map/while
  143.3 3.3 %copy-start.11 = (f32[8,10,512]{2,0,1:T(8,128)S(1)}, f32[8,10,512]{2,0,1:T(8,128)}, u32[]{:S(2)}) copy-start(f32[8,10,512]{2,0,1:T(8,128)} %get-tuple-element.245) | copy-start | bytes 491524 | tf_op jit(solution)/shard_map/while
  143.3 3.3 %copy-start.12 = (f32[8,10,512]{2,0,1:T(8,128)S(1)}, f32[8,10,512]{2,0,1:T(8,128)}, u32[]{:S(2)}) copy-start(f32[8,10,512]{2,0,1:T(8,128)} %get-tuple-element.254) | copy-start | bytes 491524 | tf_op jit(solution)/shard_map/while
  143.3 3.3 %copy-start.13 = (f32[8,10,512]{2,0,1:T(8,128)S(1)}, f32[8,10,512]{2,0,1:T(8,128)}, u32[]{:S(2)}) copy-start(f32[8,10,512]{2,0,1:T(8,128)} %get-tuple-element.243) | copy-start | bytes 491524 | tf_op jit(solution)/shard_map/while
  143.3 3.3 %copy-start.20 = (f32[1,512]{1,0:T(1,128)S(1)}, f32[1,512]{1,0:T(1,128)}, u32[]{:S(2)}) copy-start(f32[1,512]{1,0:T(1,128)} %get-tuple-element.257) | copy-start | bytes 6148 | tf_op jit(solution)/shard_map/while
  143.3 3.3 %copy-start.21 = (f32[1,512]{1,0:T(1,128)S(1)}, f32[1,512]{1,0:T(1,128)}, u32[]{:S(2)}) copy-start(f32[1,512]{1,0:T(1,128)} %get-tuple-element.259) | copy-start | bytes 6148 | tf_op jit(solution)/shard_map/while
  143.3 3.3 %copy-start.22 = (bf16[2,8,5,512]{3,1,2,0:T(8,128)(2,1)S(1)}, bf16[2,8,5,512]{3,1,2,0:T(8,128)(2,1)}, u32[]{:S(2)}) copy-start(bf16[2,8,5,512]{3,1,2,0:T(8,128)(2,1)} %get-tuple-element.272) | copy-start | bytes 245764 | tf_op jit(solution)/shard_map/while
  146.9 0.6 copy-start.23
  157.5 0.7 copy-start.1
  209.9 7.4 %copy-start.26 = (pred[512]{0:T(512)(128)(4,1)S(1)}, pred[512]{0:T(512)(128)(4,1)}, u32[]{:S(2)}) copy-start(pred[512]{0:T(512)(128)(4,1)} %compare_and_fusion.17) | copy-start | bytes 1540 | tf_op jit(solution)/shard_map/while
  217.3 7.4 %copy-start.25 = (pred[512]{0:T(512)(128)(4,1)S(1)}, pred[512]{0:T(512)(128)(4,1)}, u32[]{:S(2)}) copy-start(pred[512]{0:T(512)(128)(4,1)} %compare_and_fusion.16) | copy-start | bytes 1540 | tf_op jit(solution)/shard_map/while
  232.0 6.0 %copy-start.16 = (f32[1,512]{1,0:T(1,128)S(1)}, f32[1,512]{1,0:T(1,128)}, u32[]{:S(2)}) copy-start(f32[1,512]{1,0:T(1,128)} %get-tuple-element.261) | copy-start | bytes 6148 | tf_op jit(solution)/shard_map/while
  232.0 6.0 %copy-start.17 = (f32[1,512]{1,0:T(1,128)S(1)}, f32[1,512]{1,0:T(1,128)}, u32[]{:S(2)}) copy-start(f32[1,512]{1,0:T(1,128)} %get-tuple-element.251) | copy-start | bytes 6148 | tf_op jit(solution)/shard_map/while
  232.0 6.0 %copy-start.18 = (f32[1,512]{1,0:T(1,128)S(1)}, f32[1,512]{1,0:T(1,128)}, u32[]{:S(2)}) copy-start(f32[1,512]{1,0:T(1,128)} %get-tuple-element.253) | copy-start | bytes 6148 | tf_op jit(solution)/shard_map/while
  232.1 6.0 %copy-start.19 = (f32[1,512]{1,0:T(1,128)S(1)}, f32[1,512]{1,0:T(1,128)}, u32[]{:S(2)}) copy-start(f32[1,512]{1,0:T(1,128)} %get-tuple-element.255) | copy-start | bytes 6148 | tf_op jit(solution)/shard_map/while
  234.8 2.5 %copy-start.4 = (f32[512,8,10]{0,1,2:T(8,128)S(1)}, f32[512,8,10]{0,1,2:T(8,128)}, u32[]{:S(2)}) copy-start(f32[512,8,10]{0,1,2:T(8,128)} %copy.165) | copy-start | bytes 491524 | tf_op jit(solution)/shard_map/while
  234.8 3.2 %copy-start.3 = (f32[512,8,10]{0,1,2:T(8,128)S(1)}, f32[512,8,10]{0,1,2:T(8,128)}, u32[]{:S(2)}) copy-start(f32[512,8,10]{0,1,2:T(8,128)} %copy.167) | copy-start | bytes 491524 | tf_op jit(solution)/shard_map/while
  234.8 3.2 %copy-start.5 = (f32[512,8,10]{0,1,2:T(8,128)S(1)}, f32[512,8,10]{0,1,2:T(8,128)}, u32[]{:S(2)}) copy-start(f32[512,8,10]{0,1,2:T(8,128)} %copy.166) | copy-start | bytes 491524 | tf_op jit(solution)/shard_map/while
  234.8 3.2 %copy-start.24 = (pred[512]{0:T(512)(128)(4,1)S(1)}, pred[512]{0:T(512)(128)(4,1)}, u32[]{:S(2)}) copy-start(pred[512]{0:T(512)(128)(4,1)} %compare_and_fusion.15) | copy-start | bytes 1540 | tf_op jit(solution)/shard_map/while
  234.8 3.3 %copy-start.2 = (f32[8,5,768]{2,0,1:T(8,128)S(1)}, f32[8,5,768]{2,0,1:T(8,128)}, u32[]{:S(2)}) copy-start(f32[8,5,768]{2,0,1:T(8,128)} %copy-done.1) | copy-start | bytes 368644 | tf_op jit(solution)/shard_map/while
  234.8 3.3 %copy-start.6 = (f32[8,10,512]{2,0,1:T(8,128)S(1)}, f32[8,10,512]{2,0,1:T(8,128)}, u32[]{:S(2)}) copy-start(f32[8,10,512]{2,0,1:T(8,128)} %get-tuple-element.260) | copy-start | bytes 491524 | tf_op jit(solution)/shard_map/while
  234.8 3.3 %copy-start.7 = (f32[8,10,512]{2,0,1:T(8,128)S(1)}, f32[8,10,512]{2,0,1:T(8,128)}, u32[]{:S(2)}) copy-start(f32[8,10,512]{2,0,1:T(8,128)} %get-tuple-element.249) | copy-start | bytes 491524 | tf_op jit(solution)/shard_map/while
  234.8 3.3 %copy-start.8 = (f32[8,10,512]{2,0,1:T(8,128)S(1)}, f32[8,10,512]{2,0,1:T(8,128)}, u32[]{:S(2)}) copy-start(f32[8,10,512]{2,0,1:T(8,128)} %get-tuple-element.258) | copy-start | bytes 491524 | tf_op jit(solution)/shard_map/while
  234.8 3.3 %copy-start.9 = (f32[8,10,512]{2,0,1:T(8,128)S(1)}, f32[8,10,512]{2,0,1:T(8,128)}, u32[]{:S(2)}) copy-start(f32[8,10,512]{2,0,1:T(8,128)} %get-tuple-element.247) | copy-start | bytes 491524 | tf_op jit(solution)/shard_map/while
  234.8 3.3 %copy-start.10 = (f32[8,10,512]{2,0,1:T(8,128)S(1)}, f32[8,10,512]{2,0,1:T(8,128)}, u32[]{:S(2)}) copy-start(f32[8,10,512]{2,0,1:T(8,128)} %get-tuple-element.256) | copy-start | bytes 491524 | tf_op jit(solution)/shard_map/while
  234.8 3.3 %copy-start.11 = (f32[8,10,512]{2,0,1:T(8,128)S(1)}, f32[8,10,512]{2,0,1:T(8,128)}, u32[]{:S(2)}) copy-start(f32[8,10,512]{2,0,1:T(8,128)} %get-tuple-element.245) | copy-start | bytes 491524 | tf_op jit(solution)/shard_map/while
  234.8 3.3 %copy-start.12 = (f32[8,10,512]{2,0,1:T(8,128)S(1)}, f32[8,10,512]{2,0,1:T(8,128)}, u32[]{:S(2)}) copy-start(f32[8,10,512]{2,0,1:T(8,128)} %get-tuple-element.254) | copy-start | bytes 491524 | tf_op jit(solution)/shard_map/while
  234.9 3.3 %copy-start.13 = (f32[8,10,512]{2,0,1:T(8,128)S(1)}, f32[8,10,512]{2,0,1:T(8,128)}, u32[]{:S(2)}) copy-start(f32[8,10,512]{2,0,1:T(8,128)} %get-tuple-element.243) | copy-start | bytes 491524 | tf_op jit(solution)/shard_map/while
  234.9 3.3 %copy-start.20 = (f32[1,512]{1,0:T(1,128)S(1)}, f32[1,512]{1,0:T(1,128)}, u32[]{:S(2)}) copy-start(f32[1,512]{1,0:T(1,128)} %get-tuple-element.257) | copy-start | bytes 6148 | tf_op jit(solution)/shard_map/while
  234.9 3.3 %copy-start.21 = (f32[1,512]{1,0:T(1,128)S(1)}, f32[1,512]{1,0:T(1,128)}, u32[]{:S(2)}) copy-start(f32[1,512]{1,0:T(1,128)} %get-tuple-element.259) | copy-start | bytes 6148 | tf_op jit(solution)/shard_map/while
  234.9 3.3 %copy-start.22 = (bf16[2,8,5,512]{3,1,2,0:T(8,128)(2,1)S(1)}, bf16[2,8,5,512]{3,1,2,0:T(8,128)(2,1)}, u32[]{:S(2)}) copy-start(bf16[2,8,5,512]{3,1,2,0:T(8,128)(2,1)} %get-tuple-element.272) | copy-start | bytes 245764 | tf_op jit(solution)/shard_map/while
  238.5 0.6 copy-start.23
